TPU v7x, 32 devices: a whole 2x2x4 slice. The times are simulated.
32 devices in a mesh: groups: 2 (over x), utt: 16 (over z, y, core).
Axes of the slice: x: 2, y: 2, z: 4, core: 2. Of those that a mesh axis runs over, the one named last changes fastest.
Arguments:
- cache_kv: bfloat16 [512, 8, 3072], P(('groups', 'utt')), parts along dimension 0, may hold values from -160 to 160
- new_rows: bfloat16 [512, 4608], P(('groups', 'utt')), parts along dimension 0, may hold values from -6 to 6
- cross_queries: bfloat16 [512, 1536], P(('groups', 'utt')), parts along dimension 0, may hold values from -6 to 6
- enc_kv: bfloat16 [32, 256, 3072], P(('groups', 'utt')), parts along dimension 0, may hold values from -160 to 160
- lengths: int32 [32], P(('groups', 'utt')), parts along dimension 0, may hold values from 64 to 256, as said below
- parents: int32 [32, 16], P(('groups', 'utt')), parts along dimension 0, may hold values from 0 to 15
Outputs:
- mixed: bfloat16 [512, 1536], P(('groups', 'utt')), parts along dimension 0
There are 2 independent parts, one for each index of `groups`. A program takes and returns all parts, laid end to end along the dimension named above; each array names one. Nothing has to cross between parts.
Inputs may be any that keep to these rules, and one draw needn't show every extreme that they name: `lengths`: some utterance of each part has all 256 frames.
All inputs are finite; a program needn't handle non-finite values.
Results may differ from a plain program's by a relative error of at most 0.009.
Values may be sent and summed in bfloat16 or wider, within the bound.
A program may use at most 64 MiB of HBM per device.

v0:
```python
import functools

import jax
import jax.numpy as jnp
from jax import lax
from jax.experimental import pallas as pl
from jax.experimental.pallas import tpu as pltpu
from jax.sharding import PartitionSpec as P

HD = 128
CORES = 2
LINES = 2
PARTS = 3


def chunk_sizes(heads):
    first = heads // 3
    return [first, heads - first] if first else [heads]
LOW = -1e30


def contract_last(a, b):
    return lax.dot_general(a, b, (((1,), (1,)), ((), ())), preferred_element_type=jnp.float32)


def fast_kernel(
    n,
    cache_ref, new_ref, cq_ref, enc_ref, len_ref, par_ref,
    out_ref,
    qbuf, kbuf, vbuf, newbuf, cqbuf, encbuf, ptab, ctx, ybuf, sbuf, zbuf, xsend, xrecv,
    local_sem, q_send, q_recv, f_send, c_send, c_recv, p_send, p_recv, x_send, x_recv,
    y_send, y_recv, z_send, z_recv, qown_sem, stay_sem,
):
    feature = cq_ref.shape[1]
    half = feature // CORES
    heads = half // HD
    sizes = chunk_sizes(heads)
    chunks = len(sizes)
    starts = [sum(sizes[:k]) for k in range(chunks)]
    rows = cq_ref.shape[0]
    utts = new_ref.shape[0]
    old = cache_ref.shape[0]
    history = old // utts
    depth = n // (CORES * LINES)
    scale = HD ** (-0.5)

    me = lax.axis_index("utt")
    z = me // (CORES * LINES)
    y = (me // CORES) % LINES
    c = me % CORES
    y_other = 1 - y
    c_other = 1 - c

    def at(zz, yy, cc):
        return (zz * LINES + yy) * CORES + cc

    def remote(src, dst, ssem, rsem, dev):
        return pltpu.make_async_remote_copy(
            src_ref=src, dst_ref=dst, send_sem=ssem, recv_sem=rsem,
            device_id={"utt": dev}, device_id_type=pl.DeviceIdType.MESH,
        )

    barrier = pltpu.get_barrier_semaphore()
    for k in range(1, n):
        pl.semaphore_signal(
            barrier, inc=1, device_id={"utt": lax.rem(me + k, n)},
            device_id_type=pl.DeviceIdType.MESH,
        )

    def chunk_cols(cc, k):
        return pl.ds(pl.multiple_of(cc * half + starts[k] * HD, HD), sizes[k] * HD)

    my_half = pl.ds(pl.multiple_of(c * half, HD), half)
    my_values = pl.ds(pl.multiple_of(feature + c * half, HD), half)
    my_rows = pl.ds(pl.multiple_of(c * old, old), old)
    copies = [
        pltpu.make_async_copy(cq_ref, cqbuf, local_sem.at[0]),
        pltpu.make_async_copy(enc_ref.at[0], encbuf, local_sem.at[1]),
        pltpu.make_async_copy(new_ref, newbuf, local_sem.at[2]),
        pltpu.make_async_copy(cache_ref.at[:, my_half], kbuf.at[my_rows], local_sem.at[4]),
        pltpu.make_async_copy(cache_ref.at[:, my_values], vbuf.at[my_rows], local_sem.at[5]),
        pltpu.make_async_copy(par_ref, ptab.at[me], local_sem.at[6]),
    ] + [
        pltpu.make_async_copy(new_ref.at[:, chunk_cols(c, k)], qbuf[k].at[z, y, c], qown_sem.at[k])
        for k in range(chunks)
    ]
    for cp in copies:
        cp.start()

    copies[0].wait()
    copies[1].wait()

    frames = encbuf.shape[0]
    live = lax.broadcasted_iota(jnp.int32, (rows, frames), 1) < len_ref[0]
    ones_f = jnp.ones((frames, HD), jnp.bfloat16)

    def cross(h):
        cols = slice(h * HD, (h + 1) * HD)
        s = contract_last(cqbuf[:, cols], encbuf[:, cols]) * scale
        s = jnp.where(live, s, LOW)
        p = jnp.where(live, jnp.exp(s - jnp.max(s, axis=1, keepdims=True)), 0.0).astype(jnp.bfloat16)
        v = jnp.concatenate([encbuf[:, feature + h * HD : feature + (h + 1) * HD], ones_f], axis=1)
        o = jnp.dot(p, v, preferred_element_type=jnp.float32)
        o = o[:, :HD] / o[:, HD:]
        for b in range(rows):
            xsend[b, :, cols] = o[b : b + 1, :]

    early = (feature // HD) // 3
    for h in range(early):
        cross(h)

    copies[2].wait()
    pl.semaphore_wait(barrier, n - 1)

    sends = []

    def spread(k):
        slot = 0
        for dz in (*range(1, depth), 0):
            zz = lax.rem(z + dz, depth)
            for dc in range(CORES):
                cc = lax.rem(c + dc, CORES)
                for yy in (y_other, y) if dz == 0 else (y,):
                    if dz == 0 and dc == 0 and yy is y:
                        continue
                    cp = remote(newbuf.at[:, chunk_cols(cc, k)], qbuf[k].at[z, y, c],
                                q_send.at[k, slot], q_recv.at[k, me], at(zz, yy, cc))
                    cp.start()
                    sends.append(cp)
                    slot += 1

    spread(0)
    for k in range(1, n):
        dev = lax.rem(me + k, n)
        cp = remote(par_ref, ptab.at[me], p_send.at[k - 1], p_recv.at[me], dev)
        cp.start()
        sends.append(cp)
    for k in range(1, chunks):
        spread(k)
    other_half = pl.ds(pl.multiple_of(c_other * half, HD), half)
    other_values = pl.ds(pl.multiple_of(feature + c_other * half, HD), half)
    partner = at(z, y, c_other)
    cache_in = []
    for i, (cols, buf) in enumerate(((other_half, kbuf), (other_values, vbuf))):
        cp = remote(cache_ref.at[:, cols], buf.at[my_rows], c_send.at[i], c_recv.at[i], partner)
        cp.start()
        sends.append(cp)
        cache_in.append(cp)

    def forward(k):
        slot = 0
        for dz in range(1, depth):
            zz = lax.rem(z + dz, depth)
            for cc in range(CORES):
                src = at(zz, y, cc)
                piece = qbuf[k].at[zz, y, cc]
                remote(piece, piece, f_send.at[k, slot], q_recv.at[k, src], src).wait_recv()
                cp = remote(piece, piece, f_send.at[k, slot], q_recv.at[k, src], at(z, y_other, c))
                cp.start()
                sends.append(cp)
                slot += 1

    forward(0)

    for h in range(early, feature // HD):
        cross(h)

    own_x = pltpu.make_async_copy(xsend.at[me], xrecv.at[me], local_sem.at[7])
    own_x.start()
    copies[3].wait()
    copies[4].wait()
    for cp in cache_in:
        cp.wait_recv()
    copies[5].wait()
    for k in range(1, n):
        src = lax.rem(me + n - k, n)
        remote(par_ref, ptab.at[src], p_send.at[0], p_recv.at[src], src).wait_recv()

    table = jnp.concatenate([ptab[u] for u in range(utts)], axis=0)
    beam_lane = lax.broadcasted_iota(jnp.int32, table.shape, 1)
    row_u = lax.broadcasted_iota(jnp.int32, (utts, 1), 0)
    chip = me // CORES
    keys = CORES * old
    ones_k = jnp.ones((keys, HD), jnp.bfloat16)

    def masks(yy):
        target = []
        for zz in range(depth):
            for cc in range(CORES):
                col = jnp.sum(jnp.where(beam_lane == at(zz, yy, cc), table, 0), axis=1, keepdims=True)
                target.append((col - chip * CORES) * utts + row_u)
        target = jnp.concatenate(target, axis=0)
        valid = lax.broadcasted_iota(jnp.int32, (count, keys), 1) // history == target
        sel = jnp.broadcast_to((target >= 0) & (target < CORES * utts), (count, HD))
        return valid, sel

    count = depth * CORES * utts
    lane = lax.broadcasted_iota(jnp.int32, (count, HD), 1)

    def partial(yy, mask, stats, k):
        valid, sel = mask
        for hk in range(sizes[k]):
            h = starts[k] + hk
            cols = slice(h * HD, (h + 1) * HD)
            kcols = slice(hk * HD, (hk + 1) * HD)
            q = qbuf[k][:, pl.ds(yy, 1), :, :, kcols].reshape(count, HD)
            s = jnp.where(valid, contract_last(q, kbuf[:, cols]) * scale, LOW)
            m = jnp.max(s, axis=1, keepdims=True)
            p = jnp.where(valid, jnp.exp(s - m), 0.0).astype(jnp.bfloat16)
            v = jnp.concatenate([vbuf[:, cols], ones_k], axis=1)
            o = jnp.dot(p, v, preferred_element_type=jnp.float32)
            total = jnp.where(sel, o[:, HD:], 1.0)
            ctx[k][:, pl.ds(yy, 1), :, :, kcols] = (o[:, :HD] / total).astype(jnp.bfloat16).reshape(
                depth, 1, CORES, utts, HD)
            rest = jnp.where(sel, m + jnp.log(total), 0.0)
            for j in range(PARTS):
                part = rest.astype(jnp.bfloat16).astype(jnp.float32)
                stats = jnp.where(lane == PARTS * h + j, part, stats)
                rest = rest - part
        if k == chunks - 1:
            ctx[k][:, pl.ds(yy, 1), :, :, sizes[k] * HD:] = stats.astype(jnp.bfloat16).reshape(
                depth, 1, CORES, utts, HD)
        return stats

    across = at(z, y_other, c)
    y_in = [[] for _ in range(chunks)]

    def turn(k):
        for dz in (*range(1, depth), 0):
            zz = lax.rem(z + dz, depth)
            cp = remote(ctx[k].at[zz, y_other], ybuf[k].at[dz], y_send.at[k, dz], y_recv.at[k, dz],
                        across)
            cp.start()
            sends.append(cp)
            y_in[k].append((dz, zz, cp))

    stays = []

    def deliver(k):
        slot = 0
        for dz, zz, cp in y_in[k]:
            cp.wait_recv()
            sbuf[k][dz] = ctx[k][pl.ds(zz, 1), pl.ds(y, 1)].reshape(sbuf[k].shape[1:]) + ybuf[k][dz]
            for dc in range(CORES):
                cc = lax.rem(c + dc, CORES)
                if dz == 0 and dc == 0:
                    stay = pltpu.make_async_copy(sbuf[k].at[dz, cc], zbuf[k].at[z, c], stay_sem.at[k])
                    stay.start()
                    stays.append(stay)
                    continue
                cp = remote(sbuf[k].at[dz, cc], zbuf[k].at[z, c], z_send.at[k, slot],
                            z_recv.at[k, z * CORES + c], at(zz, y, cc))
                cp.start()
                sends.append(cp)
                slot += 1

    mask_here, mask_there = masks(y), masks(y_other)
    stats_here = stats_there = jnp.zeros((count, HD), jnp.float32)
    for k in range(chunks):
        piece = qbuf[k].at[z, y, c_other]
        remote(piece, piece, f_send.at[k, 0], q_recv.at[k, partner], partner).wait_recv()
        copies[6 + k].wait()
        if k + 1 < chunks:
            forward(k + 1)
        stats_here = partial(y, mask_here, stats_here, k)
        for zz in range(depth):
            for cc in range(CORES):
                src = at(zz, y_other, cc)
                piece = qbuf[k].at[zz, y_other, cc]
                remote(piece, piece, f_send.at[k, 0], q_recv.at[k, src], src).wait_recv()
        stats_there = partial(y_other, mask_there, stats_there, k)
        turn(k)
        if k == 0:
            for i in range(1, n):
                dev = lax.rem(me + i, n)
                cp = remote(xsend.at[dev], xrecv.at[me], x_send.at[i - 1], x_recv.at[me], dev)
                cp.start()
                sends.append(cp)
        if k > 0:
            deliver(k - 1)

    own = []
    for h in range(feature // HD):
        q = newbuf[:, h * HD : (h + 1) * HD].astype(jnp.float32)
        k = newbuf[:, feature + h * HD : feature + (h + 1) * HD].astype(jnp.float32)
        own.append(jnp.sum(q * k, axis=1, keepdims=True) * scale)

    deliver(chunks - 1)

    own_x.wait()
    for k in range(1, n):
        src = lax.rem(me + n - k, n)
        remote(xsend.at[src], xrecv.at[src], x_send.at[0], x_recv.at[src], src).wait_recv()

    for stay in stays:
        stay.wait()
    for k in range(chunks):
        for dz in range(depth):
            zz = lax.rem(z + dz, depth)
            for dc in range(CORES):
                if dz == 0 and dc == 0:
                    continue
                cc = lax.rem(c + dc, CORES)
                remote(zbuf[k].at[zz, cc], zbuf[k].at[zz, cc], z_send.at[k, 0],
                       z_recv.at[k, zz * CORES + cc], at(zz, y, cc)).wait_recv()

    for cc in range(CORES):
        both = []
        for k in range(chunks):
            both.append(zbuf[k][0, cc].astype(jnp.float32))
            for zz in range(1, depth):
                both[k] = both[k] + zbuf[k][zz, cc].astype(jnp.float32)
        both = jnp.concatenate(both, axis=1)
        stats = both[:, half:]
        lane = lax.broadcasted_iota(jnp.int32, stats.shape, 1)
        for hl in range(heads):
            h = cc * heads + hl
            cols = slice(h * HD, (h + 1) * HD)
            mine = (lane >= PARTS * hl) & (lane < PARTS * (hl + 1))
            lse = jnp.sum(jnp.where(mine, stats, 0.0), axis=1, keepdims=True)
            peak = jnp.maximum(lse, own[h])
            w_old = jnp.exp(lse - peak)
            w_own = jnp.exp(own[h] - peak)
            inv = 1.0 / (w_old + w_own)
            value = newbuf[:, 2 * feature + h * HD : 2 * feature + (h + 1) * HD].astype(jnp.float32)
            self_ctx = both[:, hl * HD : (hl + 1) * HD] * (w_old * inv) + value * (w_own * inv)
            crossed = jnp.concatenate([xrecv[u, :, cols] for u in range(utts)], axis=0)
            out_ref[:, cols] = (
                self_ctx.astype(jnp.bfloat16).astype(jnp.float32) + crossed
            ).astype(jnp.bfloat16)

    for cp in sends:
        cp.wait_send()


def fast_body(n, cache_kv, new_rows, cross_queries, enc_kv, lengths, parents):
    rows, feature = cross_queries.shape
    utts, history, width = cache_kv.shape
    half = feature // CORES
    old = utts * history
    depth = n // (CORES * LINES)
    heads = half // HD
    sizes = chunk_sizes(heads)
    chunks = len(sizes)
    wide = [v * HD for v in sizes[:-1]] + [(sizes[-1] + 1) * HD]
    frames = enc_kv.shape[1]
    bf = jnp.bfloat16
    dma = pltpu.SemaphoreType.DMA
    hbm = pl.BlockSpec(memory_space=pl.ANY)
    return pl.pallas_call(
        functools.partial(fast_kernel, n),
        out_shape=jax.ShapeDtypeStruct((utts, feature), bf),
        in_specs=[hbm, hbm, hbm, hbm, pl.BlockSpec(memory_space=pltpu.SMEM),
                  pl.BlockSpec(memory_space=pltpu.VMEM)],
        out_specs=pl.BlockSpec(memory_space=pltpu.VMEM),
        scratch_shapes=[
            [pltpu.VMEM((depth, LINES, CORES, utts, v * HD), bf) for v in sizes],
            pltpu.VMEM((CORES * old, half), bf),
            pltpu.VMEM((CORES * old, half), bf),
            pltpu.VMEM(new_rows.shape, bf),
            pltpu.VMEM(cross_queries.shape, bf),
            pltpu.VMEM((frames, width), bf),
            pltpu.VMEM((n,) + parents.shape, jnp.int32),
            [pltpu.VMEM((depth, LINES, CORES, utts, v), bf) for v in wide],
            [pltpu.VMEM((depth, CORES, utts, v), bf) for v in wide],
            [pltpu.VMEM((depth, CORES, utts, v), bf) for v in wide],
            [pltpu.VMEM((depth, CORES, utts, v), bf) for v in wide],
            pltpu.VMEM((rows, 1, feature), jnp.float32),
            pltpu.VMEM((utts, 1, feature), jnp.float32),
            dma((8,)),
            dma((chunks, depth * CORES + 1)), dma((chunks, n)), dma((chunks, (depth - 1) * CORES)),
            dma((2,)), dma((2,)),
            dma((n - 1,)), dma((n,)), dma((n - 1,)), dma((n,)),
            dma((chunks, depth)), dma((chunks, depth)),
            dma((chunks, depth * CORES - 1)), dma((chunks, depth * CORES)), dma((chunks,)), dma((chunks,)),
        ],
        compiler_params=pltpu.CompilerParams(
            collective_id=0, has_side_effects=True, vmem_limit_bytes=67043328
        ),
    )(cache_kv.reshape(old, width), new_rows, cross_queries, enc_kv, lengths, parents)


def reorder(cache_rows, parents):
    utterances, beam_width = parents.shape
    grouped = cache_rows.reshape(utterances, beam_width, cache_rows.shape[1], cache_rows.shape[2])
    picked = jax.vmap(lambda block, picks: block[picks])(grouped, parents)
    return picked.reshape(cache_rows.shape)


def attend_self(query, old_keys, old_values, new_key, new_value):
    row_count = query.shape[0]
    history = old_keys.shape[1]
    head_count = query.shape[1] // HD
    scale = HD ** (-0.5)
    query_heads = query.reshape(row_count, head_count, HD)
    key_heads = old_keys.reshape(row_count, history, head_count, HD)
    value_heads = old_values.reshape(row_count, history, head_count, HD)
    old_scores = (
        jnp.einsum("rhd,rthd->rht", query_heads, key_heads, preferred_element_type=jnp.float32)
        * scale
    )
    own_score = (
        jnp.einsum(
            "rhd,rhd->rh",
            query_heads,
            new_key.reshape(row_count, head_count, HD),
            preferred_element_type=jnp.float32,
        )
        * scale
    )
    peak = jnp.maximum(jnp.max(old_scores, axis=2), own_score)
    old_exp = jnp.exp(old_scores - peak[:, :, None])
    own_exp = jnp.exp(own_score - peak)
    total = jnp.sum(old_exp, axis=2) + own_exp
    old_weight = (old_exp / total[:, :, None]).astype(jnp.bfloat16)
    own_weight = (own_exp / total).astype(jnp.bfloat16)
    context = jnp.einsum(
        "rht,rthd->rhd", old_weight, value_heads, preferred_element_type=jnp.float32
    )
    context = context + own_weight.astype(jnp.float32)[:, :, None] * new_value.reshape(
        row_count, head_count, HD
    ).astype(jnp.float32)
    return context.reshape(row_count, head_count * HD).astype(jnp.bfloat16)


def attend_frames(queries, frames_kv, frame_counts):
    utterances = frame_counts.shape[0]
    beam_width = queries.shape[0] // utterances
    feature = queries.shape[1]
    head_count = feature // HD
    frame_total = frames_kv.shape[1]
    scale = HD ** (-0.5)
    query_heads = queries.reshape(utterances, beam_width, head_count, HD)
    key_heads = frames_kv[:, :, :feature].reshape(utterances, frame_total, head_count, HD)
    value_heads = frames_kv[:, :, feature:].reshape(utterances, frame_total, head_count, HD)
    scores = (
        jnp.einsum("ubhd,ufhd->uhbf", query_heads, key_heads, preferred_element_type=jnp.float32)
        * scale
    )
    live = (
        lax.broadcasted_iota(jnp.int32, (utterances, 1, 1, frame_total), 3)
        < frame_counts[:, None, None, None]
    )
    scores = jnp.where(live, scores, -1e30)
    peak = jnp.max(scores, axis=3, keepdims=True)
    raised = jnp.where(live, jnp.exp(scores - peak), 0.0)
    weights = (raised / jnp.sum(raised, axis=3, keepdims=True)).astype(jnp.bfloat16)
    context = jnp.einsum(
        "uhbf,ufhd->ubhd", weights, value_heads, preferred_element_type=jnp.float32
    )
    return context.reshape(utterances * beam_width, feature)


def body(cache_kv, new_rows, cross_queries, enc_kv, lengths, parents):
    feature = cross_queries.shape[1]
    cross_context = attend_frames(cross_queries, enc_kv, lengths)
    arrived, new_here = (
        lax.all_to_all(cache_kv, "utt", split_axis=0, concat_axis=0, tiled=True),
        lax.all_to_all(new_rows, "utt", split_axis=0, concat_axis=0, tiled=True),
    )
    reordered = reorder(arrived, parents)
    self_context = attend_self(
        new_here[:, :feature],
        reordered[:, :, :feature],
        reordered[:, :, feature:],
        new_here[:, feature : 2 * feature],
        new_here[:, 2 * feature :],
    )
    mixed_here = (self_context.astype(jnp.float32) + cross_context).astype(jnp.bfloat16)
    mixed = lax.all_to_all(mixed_here, "utt", split_axis=0, concat_axis=0, tiled=True)
    return mixed


def solution(mesh):
    placed = (
        P(("groups", "utt"), None, None),
        P(("groups", "utt"), None),
        P(("groups", "utt"), None),
        P(("groups", "utt"), None, None),
        P(("groups", "utt")),
        P(("groups", "utt"), None),
    )
    n = mesh.shape["utt"]

    def either(cache_kv, new_rows, cross_queries, enc_kv, lengths, parents):
        feature = cross_queries.shape[1]
        fits = (
            parents.shape == (1, n)
            and cache_kv.shape[0] == n
            and n % (CORES * LINES) == 0
            and feature % (CORES * HD) == 0
            and PARTS * (feature // (CORES * HD)) <= HD
        )
        run = functools.partial(fast_body, n) if fits else body
        return run(cache_kv, new_rows, cross_queries, enc_kv, lengths, parents)

    return jax.shard_map(
        either, mesh=mesh, in_specs=placed, out_specs=P(("groups", "utt"), None), check_vma=False
    )
```

profile of v0, /device:TPU:0, one launch (start us, length us, event | category | flops | bytes accessed | tf_op | source)
XLA Modules:
  0.0 29.6 jit_solution(18339282671132635619)
XLA Ops:
  0.7 27.5 %shard_map.64 = bf16[16,1536]{1,0:T(8,128)(2,1)} custom-call(bf16[128,3072]{1,0:T(8,128)(2,1)} %bitcast.1, bf16[16,4608]{1,0:T(8,128)(2,1)} %new_ref.1, bf16[16,1536]{1,0:T(8,128)(2,1)} %cq_ref.1, bf16[1,256,3072]{2,1,0:T(8,128)(2,1)} %enc_ref.1, s32[1]{0:T(128)S(6)} %copy.8.len_ref, s32[1,16]{1,0:T(1,128)} %par_ref.1), custom_call_target="tpu_custom_call" | custom-call | tf_op jit(solution)/shard_map/pallas_call | solution.py:350
  28.2 1.4 %copy.9 = bf16[16,1536]{1,0:T(8,128)(2,1)} copy(bf16[16,1536]{1,0:T(8,128)(2,1)} %shard_map.64) | data formatting | bytes 98304
where the time goes:
time: 29.8 us; the launch traced here: 29.6 us
  Pallas kernels  27.5 us (92%)
  local copies, waits for them, and re-layouts  1.42 us (5%)
  between operations  0.66 us (2%)
    pallas_call x1, Pallas kernels, fast_body(): pl.pallas_call(functools.partial(fast_kernel, n), out_shape=jax.ShapeDtyp...  27.5 us
    unnamed x1, local copies, waits for them, and re-layouts  1.42 us

commit v1 on v0

--- a/solution.py
+++ b/solution.py
@@ -29,7 +29,7 @@
     out_ref,
     qbuf, kbuf, vbuf, newbuf, cqbuf, encbuf, ptab, ctx, ybuf, sbuf, zbuf, xsend, xrecv,
     local_sem, q_send, q_recv, f_send, c_send, c_recv, p_send, p_recv, x_send, x_recv,
-    y_send, y_recv, z_send, z_recv, qown_sem, stay_sem,
+    y_send, y_recv, z_send, z_recv, qown_sem, stay_sem, len_smem,
 ):
     feature = cq_ref.shape[1]
     half = feature // CORES
@@ -84,14 +84,17 @@
         pltpu.make_async_copy(new_ref.at[:, chunk_cols(c, k)], qbuf[k].at[z, y, c], qown_sem.at[k])
         for k in range(chunks)
     ]
+    get_len = pltpu.make_async_copy(len_ref, len_smem, local_sem.at[3])
+    get_len.start()
     for cp in copies:
         cp.start()
 
+    get_len.wait()
     copies[0].wait()
     copies[1].wait()
 
     frames = encbuf.shape[0]
-    live = lax.broadcasted_iota(jnp.int32, (rows, frames), 1) < len_ref[0]
+    live = lax.broadcasted_iota(jnp.int32, (rows, frames), 1) < len_smem[0]
     ones_f = jnp.ones((frames, HD), jnp.bfloat16)
 
     def cross(h):
@@ -349,9 +352,8 @@
     hbm = pl.BlockSpec(memory_space=pl.ANY)
     return pl.pallas_call(
         functools.partial(fast_kernel, n),
-        out_shape=jax.ShapeDtypeStruct((utts, feature), bf),
-        in_specs=[hbm, hbm, hbm, hbm, pl.BlockSpec(memory_space=pltpu.SMEM),
-                  pl.BlockSpec(memory_space=pltpu.VMEM)],
+        out_shape=pltpu.VMEM((utts, feature), bf),
+        in_specs=[hbm, hbm, hbm, hbm, hbm, hbm],
         out_specs=pl.BlockSpec(memory_space=pltpu.VMEM),
         scratch_shapes=[
             [pltpu.VMEM((depth, LINES, CORES, utts, v * HD), bf) for v in sizes],
@@ -373,9 +375,10 @@
             dma((n - 1,)), dma((n,)), dma((n - 1,)), dma((n,)),
             dma((chunks, depth)), dma((chunks, depth)),
             dma((chunks, depth * CORES - 1)), dma((chunks, depth * CORES)), dma((chunks,)), dma((chunks,)),
+            pltpu.SMEM(lengths.shape, jnp.int32),
         ],
         compiler_params=pltpu.CompilerParams(
-            collective_id=0, has_side_effects=True, vmem_limit_bytes=67043328
+            collective_id=0, has_side_effects=True, vmem_limit_bytes=64 * 2**20 - 144 * 1024
         ),
     )(cache_kv.reshape(old, width), new_rows, cross_queries, enc_kv, lengths, parents)
 
@@ -383,8 +386,10 @@
 def reorder(cache_rows, parents):
     utterances, beam_width = parents.shape
     grouped = cache_rows.reshape(utterances, beam_width, cache_rows.shape[1], cache_rows.shape[2])
-    picked = jax.vmap(lambda block, picks: block[picks])(grouped, parents)
-    return picked.reshape(cache_rows.shape)
+    beams = lax.broadcasted_iota(jnp.int32, (1, 1, beam_width), 2)
+    pick = (parents[:, :, None] == beams).astype(cache_rows.dtype)
+    picked = jnp.einsum("ubp,uptc->ubtc", pick, grouped, preferred_element_type=jnp.float32)
+    return picked.astype(cache_rows.dtype).reshape(cache_rows.shape)
 
 
 def attend_self(query, old_keys, old_values, new_key, new_value):

time: 29.8 us -> 27.7 us (0.930)
  Pallas kernels: 27.5 us -> 26.3 us
  local copies, waits for them, and re-layouts: 1.42 us -> 0.62 us
    pallas_call x1, Pallas kernels: 27.5 us -> 26.3 us  [fast_body(): pl.pallas_call(functools.partial(fast_kernel, n), out_shape=pltpu.VMEM((u...]
    unnamed x1, local copies, waits for them, and re-layouts: 1.42 us -> 0.62 us
where the time goes in v1:
time: 27.7 us; the launch traced here: 27.5 us
  Pallas kernels  26.3 us (95%)
  between operations  0.66 us (2%)
  local copies, waits for them, and re-layouts  0.62 us (2%)
    pallas_call x1, Pallas kernels, fast_body(): pl.pallas_call(functools.partial(fast_kernel, n), out_shape=pltpu.VMEM((u...  26.3 us
    unnamed x1, local copies, waits for them, and re-layouts  0.62 us

profile of v1, /device:TPU:0, one launch (start us, length us, event | category | flops | bytes accessed | tf_op | source)
XLA Modules:
  0.0 27.5 jit_solution(15290346795211733264)
XLA Ops:
  0.7 26.3 %shard_map.64 = bf16[16,1536]{1,0:T(8,128)(2,1)S(1)} custom-call(bf16[128,3072]{1,0:T(8,128)(2,1)} %bitcast.1, bf16[16,4608]{1,0:T(8,128)(2,1)} %new_ref.1, bf16[16,1536]{1,0:T(8,128)(2,1)} %cq_ref.1, bf16[1,256,3072]{2,1,0:T(8,128)(2,1)} %enc_ref.1, s32[1]{0:T(128)S(6)} %copy.9.len_ref, s32[1,16]{1,0:T(1,128)} %par_ref.1), custom_call_target="tpu_custom_call" | custom-call | tf_op jit(solution)/shard_map/pallas_call | solution.py:353
  26.9 0.6 %copy.8 = bf16[16,1536]{1,0:T(8,128)(2,1)} copy(bf16[16,1536]{1,0:T(8,128)(2,1)S(1)} %shard_map.64) | data formatting | bytes 98304

commit v2 on v1

v2 whole, which is shorter than its diff:
```python
import functools

import jax
import jax.numpy as jnp
from jax import lax
from jax.experimental import pallas as pl
from jax.experimental.pallas import tpu as pltpu
from jax.sharding import PartitionSpec as P

HD = 128
TEAM = 4
LOW = -1e30


def contract_last(a, b):
    return lax.dot_general(a, b, (((1,), (1,)), ((), ())), preferred_element_type=jnp.float32)


def fast_kernel(
    n,
    cache_ref, new_ref, cq_ref, enc_ref, len_ref, par_ref,
    out_ref,
    qbuf, kbuf, vbuf, newbuf, cqbuf, encbuf, ptab, xsend, xrecv, cross_ctx,
    ctx, zrecv, fin, fbuf, gbuf, sstat, gstat, len_smem,
    local_sem, own_sem, p_send, p_recv, q_send, q_recv, c_send, c_recv,
    x_send, x_recv, z_send, z_recv, s_send, s_recv, f_send, f_recv, g_send, g_recv,
):
    feature = cq_ref.shape[1]
    quarter = feature // TEAM
    heads = quarter // HD
    rows = cq_ref.shape[0]
    utts = new_ref.shape[0]
    old = cache_ref.shape[0]
    history = old // utts
    depth = n // TEAM
    count = n * utts
    scale = HD ** (-0.5)

    me = lax.axis_index("utt")
    z = me // TEAM
    r = me % TEAM
    others = [k + (k + depth - z) // depth for k in range(depth - 1)]

    def remote(src, dst, ssem, rsem, dev):
        return pltpu.make_async_remote_copy(
            src_ref=src, dst_ref=dst, send_sem=ssem, recv_sem=rsem,
            device_id={"utt": dev}, device_id_type=pl.DeviceIdType.MESH,
        )

    barrier = pltpu.get_barrier_semaphore()
    for k in range(1, n):
        pl.semaphore_signal(
            barrier, inc=1, device_id={"utt": lax.rem(me + k, n)},
            device_id_type=pl.DeviceIdType.MESH,
        )

    def cols(start, size):
        return pl.ds(pl.multiple_of(start, HD), size)

    get_len = pltpu.make_async_copy(len_ref, len_smem, local_sem.at[0])
    get_cq = pltpu.make_async_copy(cq_ref, cqbuf, local_sem.at[1])
    get_enc = pltpu.make_async_copy(enc_ref.at[0], encbuf, local_sem.at[2])
    get_new = pltpu.make_async_copy(new_ref, newbuf, local_sem.at[3])
    get_par = pltpu.make_async_copy(par_ref, ptab.at[me], local_sem.at[4])
    get_q = pltpu.make_async_copy(new_ref.at[:, cols(r * quarter, quarter)], qbuf.at[me], local_sem.at[5])
    for cp in (get_len, get_cq, get_enc, get_q, get_par, get_new):
        cp.start()
    get_own = []
    for h in range(heads):
        pair = []
        for i, buf in enumerate((kbuf, vbuf)):
            cp = pltpu.make_async_copy(
                cache_ref.at[:, cols(i * feature + r * quarter + h * HD, HD)], buf.at[h, r],
                own_sem.at[2 * h + i])
            cp.start()
            pair.append(cp)
        get_own.append(pair)

    frames = encbuf.shape[0]
    ones_f = jnp.ones((frames, HD), jnp.bfloat16)

    def cross(h, live):
        hc = slice(h * HD, (h + 1) * HD)
        s = contract_last(cqbuf[:, hc], encbuf[:, hc]) * scale
        s = jnp.where(live, s, LOW)
        p = jnp.where(live, jnp.exp(s - jnp.max(s, axis=1, keepdims=True)), 0.0).astype(jnp.bfloat16)
        v = jnp.concatenate([encbuf[:, feature + h * HD : feature + (h + 1) * HD], ones_f], axis=1)
        o = jnp.dot(p, v, preferred_element_type=jnp.float32)
        o = o[:, :HD] / o[:, HD:]
        for b in range(rows):
            xsend[b, :, hc] = o[b : b + 1, :]

    pl.semaphore_wait(barrier, n - 1)

    sends = []

    def send(cp):
        cp.start()
        sends.append(cp)
        return cp

    partner = r // 2 * 2 + (1 - r % 2)
    order = [lax.rem(r + 2, TEAM), (1 - r // 2) * 2 + (1 - r % 2), partner]
    for i, rr in enumerate(order):
        send(remote(new_ref.at[:, cols(rr * quarter, quarter)], qbuf.at[me],
                    q_send.at[i], q_recv.at[me], z * TEAM + rr))
    for k, zz in enumerate(others):
        send(remote(new_ref.at[:, cols(r * quarter, quarter)], qbuf.at[me],
                    q_send.at[TEAM - 1 + k], q_recv.at[me], zz * TEAM + r))

    def give(h, i, js):
        buf = (kbuf, vbuf)[i]
        return [send(remote(cache_ref.at[:, cols(i * feature + order[j] * quarter + h * HD, HD)],
                            buf.at[h, r], c_send.at[2 * h + i, j], c_recv.at[2 * h + i, r],
                            z * TEAM + order[j])) for j in js]

    last = heads - 1
    far = tuple(range(TEAM - 2))
    first = [give(h, i, far) for h in range(last) for i in range(2)]
    for k in range(1, n):
        send(remote(par_ref, ptab.at[me], p_send.at[k - 1], p_recv.at[me], lax.rem(me + k, n)))
    for h in range(heads):
        for i in range(2):
            give(h, i, (TEAM - 2,))

    get_len.wait()
    get_cq.wait()
    get_enc.wait()
    live = lax.broadcasted_iota(jnp.int32, (rows, frames), 1) < len_smem[0]
    count_h = feature // HD

    def pass_on(i):
        src = z * TEAM + order[i]
        piece = qbuf.at[src]
        remote(piece, piece, q_send.at[0], q_recv.at[src], src).wait_recv()
        for k, zz in enumerate(others):
            send(remote(piece, piece, q_send.at[TEAM - 1 + (depth - 1) * (i + 1) + k], q_recv.at[src],
                        zz * TEAM + r))

    for h in range(count_h // 4):
        cross(h, live)
    pass_on(TEAM - 2)
    for h in range(count_h // 4, count_h // 2):
        cross(h, live)
    for i in far:
        pass_on(i)
    for h in range(count_h // 2, count_h):
        cross(h, live)
    own_x = pltpu.make_async_copy(xsend.at[me], xrecv.at[me], local_sem.at[6])
    own_x.start()

    def send_x(devs, at):
        for k, dev in enumerate(devs):
            send(remote(xsend.at[dev], xrecv.at[me], x_send.at[at + k], x_recv.at[me], dev))

    side = r // 2 * 2
    near_x = [zz * TEAM + side + c for zz in others for c in range(2)] + [z * TEAM + partner]
    far_x = [zz * TEAM + TEAM - 2 - side + c for zz in (*others, z) for c in range(2)]
    send_x(near_x, 0)

    get_par.wait()
    for k in range(1, n):
        src = lax.rem(me + n - k, n)
        remote(par_ref, ptab.at[src], p_send.at[0], p_recv.at[src], src).wait_recv()
    table = jnp.concatenate([ptab[u] for u in range(utts)], axis=0)
    beam_lane = lax.broadcasted_iota(jnp.int32, table.shape, 1)
    slot = jnp.concatenate(
        [jnp.sum(jnp.where(beam_lane == b, table, 0), axis=1, keepdims=True) for b in range(n)], axis=0)
    slot = jnp.broadcast_to(slot - z * TEAM, (count, old))
    lane = lax.broadcasted_iota(jnp.int32, (count, old), 1)
    row_u = lax.rem(lax.broadcasted_iota(jnp.int32, (count, old), 0), utts)
    own_key = lane // history == row_u
    here = (slot[:, :1] >= 0) & (slot[:, :1] < TEAM)
    spot = lane - row_u

    get_new.wait()
    own = []
    for h in range(feature // HD):
        q = newbuf[:, h * HD : (h + 1) * HD].astype(jnp.float32)
        k = newbuf[:, feature + h * HD : feature + (h + 1) * HD].astype(jnp.float32)
        own.append(jnp.sum(q * k, axis=1, keepdims=True) * scale)

    hold = []
    for i, pair in enumerate(first):
        for cp in pair:
            cp.wait_send()
            hold.append(cp)
        if i == 0:
            give(last, 0, far)
    if not first:
        give(last, 0, far)
    give(last, 1, far)

    get_q.wait()
    for zz in others:
        for t in range(TEAM):
            src = zz * TEAM + t
            piece = qbuf.at[src]
            remote(piece, piece, q_send.at[0], q_recv.at[src], src).wait_recv()

    def arrive(h, i):
        get_own[h][i].wait()
        buf = (kbuf, vbuf)[i]
        for rr in order:
            remote(buf.at[h, rr], buf.at[h, rr], c_send.at[2 * h + i, 0], c_recv.at[2 * h + i, rr],
                   z * TEAM + rr).wait_recv()

    def deliver(h):
        total = ctx[h, pl.ds(z, 1)].reshape(TEAM, utts, HD)
        for zz in others:
            remote(zrecv.at[h, zz], zrecv.at[h, zz], z_send.at[h, 0], z_recv.at[h, zz],
                   zz * TEAM + r).wait_recv()
            total = total + zrecv[h, pl.ds(zz, 1)].reshape(TEAM, utts, HD)
        fin[h] = total
        for i, rr in enumerate(order):
            send(remote(fin.at[h, rr], fbuf.at[r, h], f_send.at[h, i], f_recv.at[r, h], z * TEAM + rr))
        fbuf[pl.ds(r, 1), h] = fin[h, pl.ds(r, 1)]

    team = [(zz, rr) for zz in others for rr in (r, partner, order[0], order[1])]
    team += [(z, rr) for rr in order]
    stats = jnp.zeros((count, HD), jnp.float32)
    for h in range(heads):
        arrive(h, 0)
        q = qbuf[:, :, h * HD : (h + 1) * HD].reshape(count, HD)
        s = contract_last(q, kbuf[h].reshape(TEAM * old, HD))
        picked = s[:, :old]
        for t in range(1, TEAM):
            picked = jnp.where(slot == t, s[:, t * old : (t + 1) * old], picked)
        picked = jnp.where(own_key, picked * scale, LOW)
        m = jnp.max(picked, axis=1, keepdims=True)
        e = jnp.where(own_key, jnp.exp(picked - m), 0.0)
        total = jnp.sum(e, axis=1, keepdims=True)
        e = e * (1.0 / total)
        p = jnp.concatenate(
            [jnp.where(slot == t, e, 0.0).astype(jnp.bfloat16) for t in range(TEAM)], axis=1)
        stats = jnp.where(spot == h * utts, jnp.where(here, m + jnp.log(total), 0.0), stats)
        if h == last:
            for g in range(n):
                sstat[g] = jnp.sum(stats[g * utts : (g + 1) * utts], axis=0, keepdims=True)
            for k, (zz, rr) in enumerate(team):
                send(remote(sstat.at[zz * TEAM + rr], gstat.at[me], s_send.at[k], s_recv.at[me],
                            zz * TEAM + rr))
        arrive(h, 1)
        o = jnp.dot(p, vbuf[h].reshape(TEAM * old, HD), preferred_element_type=jnp.float32)
        ctx[h] = o.astype(jnp.bfloat16).reshape(depth, TEAM, utts, HD)
        if h == last:
            for k, (zz, rr) in enumerate(team):
                send(remote(ctx.at[h, zz, rr], gbuf.at[me], g_send.at[k], g_recv.at[me], zz * TEAM + rr))
        else:
            for k, zz in enumerate(others):
                send(remote(ctx.at[h, zz], zrecv.at[h, z], z_send.at[h, k], z_recv.at[h, z], zz * TEAM + r))
        if h == max(last - 1, 0):
            send_x(far_x, len(near_x))

    for h in range(last):
        deliver(h)
    gbuf[pl.ds(me, 1)] = ctx[last, pl.ds(z, 1), pl.ds(r, 1)].reshape(1, utts, HD)
    gstat[pl.ds(me, 1)] = sstat[pl.ds(me, 1)]

    own_x.wait()
    for k in range(1, n):
        src = lax.rem(me + n - k, n)
        remote(xsend.at[src], xrecv.at[src], x_send.at[0], x_recv.at[src], src).wait_recv()
    for h in range(feature // HD):
        hc = slice(h * HD, (h + 1) * HD)
        cross_ctx[:, hc] = jnp.concatenate([xrecv[u, :, hc] for u in range(utts)], axis=0)

    for k in range(1, n):
        src = lax.rem(me + n - k, n)
        remote(gstat.at[src], gstat.at[src], s_send.at[0], s_recv.at[src], src).wait_recv()
    weights = []
    f_lane = lax.broadcasted_iota(jnp.int32, (utts, HD), 1)
    f_row = lax.broadcasted_iota(jnp.int32, (utts, HD), 0)
    for t in range(TEAM):
        packed = gstat[t]
        for zz in range(1, depth):
            packed = packed + gstat[zz * TEAM + t]
        packed = jnp.broadcast_to(packed, (utts, HD))
        for hl in range(heads):
            lse = jnp.sum(jnp.where(f_lane == f_row + hl * utts, packed, 0.0), axis=1, keepdims=True)
            mine = own[t * heads + hl]
            peak = jnp.maximum(lse, mine)
            w_old = jnp.exp(lse - peak)
            w_own = jnp.exp(mine - peak)
            inv = 1.0 / (w_old + w_own)
            weights.append((w_old * inv, w_own * inv))

    def write(t, hl, got):
        h = t * heads + hl
        hc = slice(h * HD, (h + 1) * HD)
        w_old, w_own = weights[h]
        value = newbuf[:, 2 * feature + h * HD : 2 * feature + (h + 1) * HD].astype(jnp.float32)
        self_ctx = got.astype(jnp.float32) * w_old + value * w_own
        out_ref[:, hc] = (
            self_ctx.astype(jnp.bfloat16).astype(jnp.float32) + cross_ctx[:, hc]
        ).astype(jnp.bfloat16)

    for h in range(last):
        for rr in order:
            remote(fbuf.at[rr, h], fbuf.at[rr, h], f_send.at[h, 0], f_recv.at[rr, h],
                   z * TEAM + rr).wait_recv()
        for t in range(TEAM):
            write(t, h, fbuf[t, h])
    for k in range(1, n):
        src = lax.rem(me + n - k, n)
        remote(gbuf.at[src], gbuf.at[src], g_send.at[0], g_recv.at[src], src).wait_recv()
    for t in range(TEAM):
        got = gbuf[t]
        for zz in range(1, depth):
            got = got + gbuf[zz * TEAM + t]
        write(t, last, got)

    for cp in sends:
        if not any(cp is held for held in hold):
            cp.wait_send()


def fast_body(n, cache_kv, new_rows, cross_queries, enc_kv, lengths, parents):
    rows, feature = cross_queries.shape
    utts, history, width = cache_kv.shape
    old = utts * history
    depth = n // TEAM
    quarter = feature // TEAM
    heads = quarter // HD
    frames = enc_kv.shape[1]
    bf, f32 = jnp.bfloat16, jnp.float32
    dma = pltpu.SemaphoreType.DMA
    hbm = pl.BlockSpec(memory_space=pl.ANY)
    return pl.pallas_call(
        functools.partial(fast_kernel, n),
        out_shape=pltpu.VMEM((utts, feature), bf),
        in_specs=[hbm] * 6,
        out_specs=pl.BlockSpec(memory_space=pltpu.VMEM),
        scratch_shapes=[
            pltpu.VMEM((n, utts, quarter), bf),
            pltpu.VMEM((heads, TEAM, old, HD), bf),
            pltpu.VMEM((heads, TEAM, old, HD), bf),
            pltpu.VMEM(new_rows.shape, bf),
            pltpu.VMEM(cross_queries.shape, bf),
            pltpu.VMEM((frames, width), bf),
            pltpu.VMEM((n,) + parents.shape, jnp.int32),
            pltpu.VMEM((rows, 1, feature), f32),
            pltpu.VMEM((utts, 1, feature), f32),
            pltpu.VMEM((utts, feature), f32),
            pltpu.VMEM((heads, depth, TEAM, utts, HD), bf),
            pltpu.VMEM((heads, depth, TEAM, utts, HD), bf),
            pltpu.VMEM((heads, TEAM, utts, HD), bf),
            pltpu.VMEM((TEAM, heads, utts, HD), bf),
            pltpu.VMEM((n, utts, HD), bf),
            pltpu.VMEM((n, 1, HD), f32),
            pltpu.VMEM((n, 1, HD), f32),
            pltpu.SMEM(lengths.shape, jnp.int32),
            dma((7,)), dma((2 * heads,)), dma((n - 1,)), dma((n,)),
            dma((TEAM - 1 + TEAM * (depth - 1),)), dma((n,)),
            dma((2 * heads, TEAM - 1)), dma((2 * heads, TEAM)),
            dma((n - 1,)), dma((n,)),
            dma((heads, depth - 1)), dma((heads, depth)), dma((n - 1,)), dma((n,)),
            dma((heads, TEAM - 1)), dma((TEAM, heads)), dma((n - 1,)), dma((n,)),
        ],
        compiler_params=pltpu.CompilerParams(
            collective_id=0, has_side_effects=True, vmem_limit_bytes=64 * 2**20 - 144 * 1024
        ),
    )(cache_kv.reshape(old, width), new_rows, cross_queries, enc_kv, lengths, parents)


def reorder(cache_rows, parents):
    utterances, beam_width = parents.shape
    grouped = cache_rows.reshape(utterances, beam_width, cache_rows.shape[1], cache_rows.shape[2])
    beams = lax.broadcasted_iota(jnp.int32, (1, 1, beam_width), 2)
    pick = (parents[:, :, None] == beams).astype(cache_rows.dtype)
    picked = jnp.einsum("ubp,uptc->ubtc", pick, grouped, preferred_element_type=jnp.float32)
    return picked.astype(cache_rows.dtype).reshape(cache_rows.shape)


def attend_self(query, old_keys, old_values, new_key, new_value):
    row_count = query.shape[0]
    history = old_keys.shape[1]
    head_count = query.shape[1] // HD
    scale = HD ** (-0.5)
    query_heads = query.reshape(row_count, head_count, HD)
    key_heads = old_keys.reshape(row_count, history, head_count, HD)
    value_heads = old_values.reshape(row_count, history, head_count, HD)
    old_scores = (
        jnp.einsum("rhd,rthd->rht", query_heads, key_heads, preferred_element_type=jnp.float32)
        * scale
    )
    own_score = (
        jnp.einsum(
            "rhd,rhd->rh",
            query_heads,
            new_key.reshape(row_count, head_count, HD),
            preferred_element_type=jnp.float32,
        )
        * scale
    )
    peak = jnp.maximum(jnp.max(old_scores, axis=2), own_score)
    old_exp = jnp.exp(old_scores - peak[:, :, None])
    own_exp = jnp.exp(own_score - peak)
    total = jnp.sum(old_exp, axis=2) + own_exp
    old_weight = (old_exp / total[:, :, None]).astype(jnp.bfloat16)
    own_weight = (own_exp / total).astype(jnp.bfloat16)
    context = jnp.einsum(
        "rht,rthd->rhd", old_weight, value_heads, preferred_element_type=jnp.float32
    )
    context = context + own_weight.astype(jnp.float32)[:, :, None] * new_value.reshape(
        row_count, head_count, HD
    ).astype(jnp.float32)
    return context.reshape(row_count, head_count * HD).astype(jnp.bfloat16)


def attend_frames(queries, frames_kv, frame_counts):
    utterances = frame_counts.shape[0]
    beam_width = queries.shape[0] // utterances
    feature = queries.shape[1]
    head_count = feature // HD
    frame_total = frames_kv.shape[1]
    scale = HD ** (-0.5)
    query_heads = queries.reshape(utterances, beam_width, head_count, HD)
    key_heads = frames_kv[:, :, :feature].reshape(utterances, frame_total, head_count, HD)
    value_heads = frames_kv[:, :, feature:].reshape(utterances, frame_total, head_count, HD)
    scores = (
        jnp.einsum("ubhd,ufhd->uhbf", query_heads, key_heads, preferred_element_type=jnp.float32)
        * scale
    )
    live = (
        lax.broadcasted_iota(jnp.int32, (utterances, 1, 1, frame_total), 3)
        < frame_counts[:, None, None, None]
    )
    scores = jnp.where(live, scores, -1e30)
    peak = jnp.max(scores, axis=3, keepdims=True)
    raised = jnp.where(live, jnp.exp(scores - peak), 0.0)
    weights = (raised / jnp.sum(raised, axis=3, keepdims=True)).astype(jnp.bfloat16)
    context = jnp.einsum(
        "uhbf,ufhd->ubhd", weights, value_heads, preferred_element_type=jnp.float32
    )
    return context.reshape(utterances * beam_width, feature)


def body(cache_kv, new_rows, cross_queries, enc_kv, lengths, parents):
    feature = cross_queries.shape[1]
    cross_context = attend_frames(cross_queries, enc_kv, lengths)
    arrived, new_here = (
        lax.all_to_all(cache_kv, "utt", split_axis=0, concat_axis=0, tiled=True),
        lax.all_to_all(new_rows, "utt", split_axis=0, concat_axis=0, tiled=True),
    )
    reordered = reorder(arrived, parents)
    self_context = attend_self(
        new_here[:, :feature],
        reordered[:, :, :feature],
        reordered[:, :, feature:],
        new_here[:, feature : 2 * feature],
        new_here[:, 2 * feature :],
    )
    mixed_here = (self_context.astype(jnp.float32) + cross_context).astype(jnp.bfloat16)
    mixed = lax.all_to_all(mixed_here, "utt", split_axis=0, concat_axis=0, tiled=True)
    return mixed


def solution(mesh):
    placed = (
        P(("groups", "utt"), None, None),
        P(("groups", "utt"), None),
        P(("groups", "utt"), None),
        P(("groups", "utt"), None, None),
        P(("groups", "utt")),
        P(("groups", "utt"), None),
    )
    n = mesh.shape["utt"]

    def either(cache_kv, new_rows, cross_queries, enc_kv, lengths, parents):
        feature = cross_queries.shape[1]
        fits = (
            parents.shape == (1, n)
            and cache_kv.shape[0] == n
            and n % TEAM == 0
            and n > TEAM
            and feature % (TEAM * HD) == 0
            and cache_kv.shape[0] * cache_kv.shape[1] == HD
            and feature // (TEAM * HD) * n <= HD
        )
        run = functools.partial(fast_body, n) if fits else body
        return run(cache_kv, new_rows, cross_queries, enc_kv, lengths, parents)

    return jax.shard_map(
        either, mesh=mesh, in_specs=placed, out_specs=P(("groups", "utt"), None), check_vma=False
    )
```

time: 27.7 us -> 27 us (0.975)
  Pallas kernels: 26.3 us -> 25.6 us
    pallas_call x1, Pallas kernels: 26.3 us -> 25.6 us  [fast_body(): pl.pallas_call(functools.partial(fast_kernel, n), out_shape=pltpu.VMEM((u...]
where the time goes in v2:
time: 27 us; the launch traced here: 26.9 us
  Pallas kernels  25.6 us (95%)
  between operations  0.66 us (2%)
  local copies, waits for them, and re-layouts  0.62 us (2%)
    pallas_call x1, Pallas kernels, fast_body(): pl.pallas_call(functools.partial(fast_kernel, n), out_shape=pltpu.VMEM((u...  25.6 us
    unnamed x1, local copies, waits for them, and re-layouts  0.62 us

profile of v2, /device:TPU:0, one launch (start us, length us, event | category | flops | bytes accessed | tf_op | source)
XLA Modules:
  0.0 26.9 jit_solution(616930372343738500)
XLA Ops:
  0.7 25.6 %shard_map.64 = bf16[16,1536]{1,0:T(8,128)(2,1)S(1)} custom-call(bf16[128,3072]{1,0:T(8,128)(2,1)} %bitcast.1, bf16[16,4608]{1,0:T(8,128)(2,1)} %new_ref.1, bf16[16,1536]{1,0:T(8,128)(2,1)} %cq_ref.1, bf16[1,256,3072]{2,1,0:T(8,128)(2,1)} %enc_ref.1, s32[1]{0:T(128)S(6)} %copy.9.len_ref, s32[1,16]{1,0:T(1,128)} %par_ref.1), custom_call_target="tpu_custom_call" | custom-call | tf_op jit(solution)/shard_map/pallas_call | solution.py:329
  26.2 0.6 %copy.8 = bf16[16,1536]{1,0:T(8,128)(2,1)} copy(bf16[16,1536]{1,0:T(8,128)(2,1)S(1)} %shard_map.64) | data formatting | bytes 98304

commit v3 on v2

--- a/solution.py
+++ b/solution.py
@@ -9,6 +9,7 @@
 
 HD = 128
 TEAM = 4
+CORES = 2
 LOW = -1e30
 
 
@@ -21,9 +22,9 @@
     cache_ref, new_ref, cq_ref, enc_ref, len_ref, par_ref,
     out_ref,
     qbuf, kbuf, vbuf, newbuf, cqbuf, encbuf, ptab, xsend, xrecv, cross_ctx,
-    ctx, zrecv, fin, fbuf, gbuf, sstat, gstat, len_smem,
+    ctx, gbuf, sstat, gstat, len_smem,
     local_sem, own_sem, p_send, p_recv, q_send, q_recv, c_send, c_recv,
-    x_send, x_recv, z_send, z_recv, s_send, s_recv, f_send, f_recv, g_send, g_recv,
+    x_send, x_recv, s_send, s_recv, g_send, g_recv, ready,
 ):
     feature = cq_ref.shape[1]
     quarter = feature // TEAM
@@ -47,12 +48,23 @@
             device_id={"utt": dev}, device_id_type=pl.DeviceIdType.MESH,
         )
 
+    core = r % CORES
+    partner = r + 1 - 2 * core
+    order = [lax.rem(r + CORES, TEAM), lax.rem(partner + CORES, TEAM), partner]
+
+    def tell(sem, dev):
+        pl.semaphore_signal(sem, inc=1, device_id={"utt": dev}, device_id_type=pl.DeviceIdType.MESH)
+
     barrier = pltpu.get_barrier_semaphore()
-    for k in range(1, n):
-        pl.semaphore_signal(
-            barrier, inc=1, device_id={"utt": lax.rem(me + k, n)},
-            device_id_type=pl.DeviceIdType.MESH,
-        )
+    tell(barrier, z * TEAM + lax.rem(r - core + CORES, TEAM))
+
+    @pl.when(core == 1)
+    def _():
+        tell(barrier, z * TEAM + partner)
+
+    for zz in others:
+        for t in range(1, TEAM, CORES):
+            tell(barrier, zz * TEAM + t)
 
     def cols(start, size):
         return pl.ds(pl.multiple_of(start, HD), size)
@@ -79,6 +91,8 @@
     frames = encbuf.shape[0]
     ones_f = jnp.ones((frames, HD), jnp.bfloat16)
 
+    crossed = []
+
     def cross(h, live):
         hc = slice(h * HD, (h + 1) * HD)
         s = contract_last(cqbuf[:, hc], encbuf[:, hc]) * scale
@@ -86,11 +100,16 @@
         p = jnp.where(live, jnp.exp(s - jnp.max(s, axis=1, keepdims=True)), 0.0).astype(jnp.bfloat16)
         v = jnp.concatenate([encbuf[:, feature + h * HD : feature + (h + 1) * HD], ones_f], axis=1)
         o = jnp.dot(p, v, preferred_element_type=jnp.float32)
-        o = o[:, :HD] / o[:, HD:]
-        for b in range(rows):
-            xsend[b, :, hc] = o[b : b + 1, :]
-
-    pl.semaphore_wait(barrier, n - 1)
+        crossed.append((o[:, :HD] / o[:, HD:]).astype(jnp.bfloat16))
+
+    @pl.when(core == 0)
+    def _():
+        pl.semaphore_wait(barrier, TEAM - 1)
+        tell(ready, z * TEAM + partner)
+
+    @pl.when(core == 1)
+    def _():
+        pl.semaphore_wait(ready, 1)
 
     sends = []
 
@@ -99,14 +118,14 @@
         sends.append(cp)
         return cp
 
-    partner = r // 2 * 2 + (1 - r % 2)
-    order = [lax.rem(r + 2, TEAM), (1 - r // 2) * 2 + (1 - r % 2), partner]
-    for i, rr in enumerate(order):
-        send(remote(new_ref.at[:, cols(rr * quarter, quarter)], qbuf.at[me],
-                    q_send.at[i], q_recv.at[me], z * TEAM + rr))
-    for k, zz in enumerate(others):
-        send(remote(new_ref.at[:, cols(r * quarter, quarter)], qbuf.at[me],
-                    q_send.at[TEAM - 1 + k], q_recv.at[me], zz * TEAM + r))
+    far = tuple(range(TEAM - 2))
+    def ask(i):
+        send(remote(new_ref.at[:, cols(order[i] * quarter, quarter)], qbuf.at[me],
+                    q_send.at[i], q_recv.at[me], z * TEAM + order[i]))
+        send(remote(par_ref, ptab.at[me], p_send.at[i], p_recv.at[me], z * TEAM + order[i]))
+
+    for i in range(TEAM - 1):
+        ask(i)
 
     def give(h, i, js):
         buf = (kbuf, vbuf)[i]
@@ -115,10 +134,13 @@
                             z * TEAM + order[j])) for j in js]
 
     last = heads - 1
-    far = tuple(range(TEAM - 2))
-    first = [give(h, i, far) for h in range(last) for i in range(2)]
-    for k in range(1, n):
-        send(remote(par_ref, ptab.at[me], p_send.at[k - 1], p_recv.at[me], lax.rem(me + k, n)))
+    give(0, 0, far)
+    give(0, 1, far)
+    stream = [(h, i) for i in range(2) for h in range(1, heads)]
+    if heads > 2:
+        stream = [(1, 0), (2, 0), (1, 1), (2, 1)] + [(h, i) for h in range(3, heads) for i in range(2)]
+    for h, i in stream:
+        give(h, i, far)
     for h in range(heads):
         for i in range(2):
             give(h, i, (TEAM - 2,))
@@ -133,12 +155,28 @@
         src = z * TEAM + order[i]
         piece = qbuf.at[src]
         remote(piece, piece, q_send.at[0], q_recv.at[src], src).wait_recv()
+        remote(par_ref, ptab.at[src], p_send.at[0], p_recv.at[src], src).wait_recv()
         for k, zz in enumerate(others):
-            send(remote(piece, piece, q_send.at[TEAM - 1 + (depth - 1) * (i + 1) + k], q_recv.at[src],
-                        zz * TEAM + r))
+            spot = TEAM - 1 + (depth - 1) * (i + 1) + k
+            send(remote(piece, piece, q_send.at[spot], q_recv.at[src], zz * TEAM + r))
+            send(remote(ptab.at[src], ptab.at[src], p_send.at[spot], p_recv.at[src], zz * TEAM + r))
 
     for h in range(count_h // 4):
         cross(h, live)
+
+    @pl.when(core == 1)
+    def _():
+        pl.semaphore_wait(barrier, n - TEAM)
+        tell(ready, z * TEAM + partner)
+
+    @pl.when(core == 0)
+    def _():
+        pl.semaphore_wait(ready, 1)
+
+    for k, zz in enumerate(others):
+        send(remote(new_ref.at[:, cols(r * quarter, quarter)], qbuf.at[me],
+                    q_send.at[TEAM - 1 + k], q_recv.at[me], zz * TEAM + r))
+        send(remote(par_ref, ptab.at[me], p_send.at[TEAM - 1 + k], p_recv.at[me], zz * TEAM + r))
     pass_on(TEAM - 2)
     for h in range(count_h // 4, count_h // 2):
         cross(h, live)
@@ -146,6 +184,13 @@
         pass_on(i)
     for h in range(count_h // 2, count_h):
         cross(h, live)
+    pad = xsend.shape[1]
+    to_row = lax.broadcasted_iota(jnp.int32, (rows * pad, rows * count_h), 0)
+    from_row = lax.broadcasted_iota(jnp.int32, (rows * pad, rows * count_h), 1)
+    turn = (to_row // pad == from_row % rows) & (to_row % pad == from_row // rows)
+    turned = jnp.dot(turn.astype(jnp.bfloat16), jnp.concatenate(crossed, axis=0),
+                     preferred_element_type=jnp.float32)
+    xsend[...] = turned.astype(jnp.bfloat16).reshape(xsend.shape)
     own_x = pltpu.make_async_copy(xsend.at[me], xrecv.at[me], local_sem.at[6])
     own_x.start()
 
@@ -157,11 +202,13 @@
     near_x = [zz * TEAM + side + c for zz in others for c in range(2)] + [z * TEAM + partner]
     far_x = [zz * TEAM + TEAM - 2 - side + c for zz in (*others, z) for c in range(2)]
     send_x(near_x, 0)
+    send_x(far_x, len(near_x))
 
     get_par.wait()
-    for k in range(1, n):
-        src = lax.rem(me + n - k, n)
-        remote(par_ref, ptab.at[src], p_send.at[0], p_recv.at[src], src).wait_recv()
+    for zz in others:
+        for t in range(TEAM):
+            src = zz * TEAM + t
+            remote(par_ref, ptab.at[src], p_send.at[0], p_recv.at[src], src).wait_recv()
     table = jnp.concatenate([ptab[u] for u in range(utts)], axis=0)
     beam_lane = lax.broadcasted_iota(jnp.int32, table.shape, 1)
     slot = jnp.concatenate(
@@ -180,17 +227,6 @@
         k = newbuf[:, feature + h * HD : feature + (h + 1) * HD].astype(jnp.float32)
         own.append(jnp.sum(q * k, axis=1, keepdims=True) * scale)
 
-    hold = []
-    for i, pair in enumerate(first):
-        for cp in pair:
-            cp.wait_send()
-            hold.append(cp)
-        if i == 0:
-            give(last, 0, far)
-    if not first:
-        give(last, 0, far)
-    give(last, 1, far)
-
     get_q.wait()
     for zz in others:
         for t in range(TEAM):
@@ -205,21 +241,12 @@
             remote(buf.at[h, rr], buf.at[h, rr], c_send.at[2 * h + i, 0], c_recv.at[2 * h + i, rr],
                    z * TEAM + rr).wait_recv()
 
-    def deliver(h):
-        total = ctx[h, pl.ds(z, 1)].reshape(TEAM, utts, HD)
-        for zz in others:
-            remote(zrecv.at[h, zz], zrecv.at[h, zz], z_send.at[h, 0], z_recv.at[h, zz],
-                   zz * TEAM + r).wait_recv()
-            total = total + zrecv[h, pl.ds(zz, 1)].reshape(TEAM, utts, HD)
-        fin[h] = total
-        for i, rr in enumerate(order):
-            send(remote(fin.at[h, rr], fbuf.at[r, h], f_send.at[h, i], f_recv.at[r, h], z * TEAM + rr))
-        fbuf[pl.ds(r, 1), h] = fin[h, pl.ds(r, 1)]
-
     team = [(zz, rr) for zz in others for rr in (r, partner, order[0], order[1])]
     team += [(z, rr) for rr in order]
     stats = jnp.zeros((count, HD), jnp.float32)
-    for h in range(heads):
+    weight = []
+
+    def score(h):
         arrive(h, 0)
         q = qbuf[:, :, h * HD : (h + 1) * HD].reshape(count, HD)
         s = contract_last(q, kbuf[h].reshape(TEAM * old, HD))
@@ -231,39 +258,41 @@
         e = jnp.where(own_key, jnp.exp(picked - m), 0.0)
         total = jnp.sum(e, axis=1, keepdims=True)
         e = e * (1.0 / total)
-        p = jnp.concatenate(
-            [jnp.where(slot == t, e, 0.0).astype(jnp.bfloat16) for t in range(TEAM)], axis=1)
-        stats = jnp.where(spot == h * utts, jnp.where(here, m + jnp.log(total), 0.0), stats)
-        if h == last:
-            for g in range(n):
-                sstat[g] = jnp.sum(stats[g * utts : (g + 1) * utts], axis=0, keepdims=True)
-            for k, (zz, rr) in enumerate(team):
-                send(remote(sstat.at[zz * TEAM + rr], gstat.at[me], s_send.at[k], s_recv.at[me],
-                            zz * TEAM + rr))
+        weight.append(jnp.concatenate(
+            [jnp.where(slot == t, e, 0.0).astype(jnp.bfloat16) for t in range(TEAM)], axis=1))
+        return jnp.where(spot == h * utts, jnp.where(here, m + jnp.log(total), 0.0), stats)
+
+    def give_back(h):
         arrive(h, 1)
-        o = jnp.dot(p, vbuf[h].reshape(TEAM * old, HD), preferred_element_type=jnp.float32)
+        o = jnp.dot(weight[h], vbuf[h].reshape(TEAM * old, HD), preferred_element_type=jnp.float32)
         ctx[h] = o.astype(jnp.bfloat16).reshape(depth, TEAM, utts, HD)
-        if h == last:
-            for k, (zz, rr) in enumerate(team):
-                send(remote(ctx.at[h, zz, rr], gbuf.at[me], g_send.at[k], g_recv.at[me], zz * TEAM + rr))
-        else:
-            for k, zz in enumerate(others):
-                send(remote(ctx.at[h, zz], zrecv.at[h, z], z_send.at[h, k], z_recv.at[h, z], zz * TEAM + r))
-        if h == max(last - 1, 0):
-            send_x(far_x, len(near_x))
-
-    for h in range(last):
-        deliver(h)
-    gbuf[pl.ds(me, 1)] = ctx[last, pl.ds(z, 1), pl.ds(r, 1)].reshape(1, utts, HD)
+        for k, (zz, rr) in enumerate(team):
+            send(remote(ctx.at[h, zz, rr], gbuf.at[h, me], g_send.at[h, k], g_recv.at[h, me],
+                        zz * TEAM + rr))
+        gbuf[h, pl.ds(me, 1)] = ctx[h, pl.ds(z, 1), pl.ds(r, 1)].reshape(1, utts, HD)
+
+    stats = score(0)
+    give_back(0)
+    for h in range(1, heads):
+        stats = score(h)
+    for g in range(n):
+        sstat[g] = jnp.sum(stats[g * utts : (g + 1) * utts], axis=0, keepdims=True)
+    for k, (zz, rr) in enumerate(team):
+        send(remote(sstat.at[zz * TEAM + rr], gstat.at[me], s_send.at[k], s_recv.at[me], zz * TEAM + rr))
+    for h in range(1, heads):
+        give_back(h)
+
     gstat[pl.ds(me, 1)] = sstat[pl.ds(me, 1)]
 
     own_x.wait()
     for k in range(1, n):
         src = lax.rem(me + n - k, n)
         remote(xsend.at[src], xrecv.at[src], x_send.at[0], x_recv.at[src], src).wait_recv()
-    for h in range(feature // HD):
-        hc = slice(h * HD, (h + 1) * HD)
-        cross_ctx[:, hc] = jnp.concatenate([xrecv[u, :, hc] for u in range(utts)], axis=0)
+    to_row = lax.broadcasted_iota(jnp.int32, (utts * count_h, utts * pad), 0)
+    from_row = lax.broadcasted_iota(jnp.int32, (utts * count_h, utts * pad), 1)
+    turn = (to_row % utts == from_row // pad) & (to_row // utts == from_row % pad)
+    cross_ctx[...] = jnp.dot(turn.astype(jnp.bfloat16), xrecv[...].reshape(utts * pad, HD),
+                             preferred_element_type=jnp.float32)
 
     for k in range(1, n):
         src = lax.rem(me + n - k, n)
@@ -285,34 +314,28 @@
             inv = 1.0 / (w_old + w_own)
             weights.append((w_old * inv, w_own * inv))
 
-    def write(t, hl, got):
+    def write(t, hl):
         h = t * heads + hl
         hc = slice(h * HD, (h + 1) * HD)
+        got = gbuf[hl, t]
+        for zz in range(1, depth):
+            got = got + gbuf[hl, zz * TEAM + t]
         w_old, w_own = weights[h]
         value = newbuf[:, 2 * feature + h * HD : 2 * feature + (h + 1) * HD].astype(jnp.float32)
         self_ctx = got.astype(jnp.float32) * w_old + value * w_own
         out_ref[:, hc] = (
-            self_ctx.astype(jnp.bfloat16).astype(jnp.float32) + cross_ctx[:, hc]
+            self_ctx.astype(jnp.bfloat16).astype(jnp.float32) + cross_ctx[h * utts : (h + 1) * utts]
         ).astype(jnp.bfloat16)
 
-    for h in range(last):
-        for rr in order:
-            remote(fbuf.at[rr, h], fbuf.at[rr, h], f_send.at[h, 0], f_recv.at[rr, h],
-                   z * TEAM + rr).wait_recv()
+    for hl in range(heads):
+        for k in range(1, n):
+            src = lax.rem(me + n - k, n)
+            remote(gbuf.at[hl, src], gbuf.at[hl, src], g_send.at[hl, 0], g_recv.at[hl, src], src).wait_recv()
         for t in range(TEAM):
-            write(t, h, fbuf[t, h])
-    for k in range(1, n):
-        src = lax.rem(me + n - k, n)
-        remote(gbuf.at[src], gbuf.at[src], g_send.at[0], g_recv.at[src], src).wait_recv()
-    for t in range(TEAM):
-        got = gbuf[t]
-        for zz in range(1, depth):
-            got = got + gbuf[zz * TEAM + t]
-        write(t, last, got)
+            write(t, hl)
 
     for cp in sends:
-        if not any(cp is held for held in hold):
-            cp.wait_send()
+        cp.wait_send()
 
 
 def fast_body(n, cache_kv, new_rows, cross_queries, enc_kv, lengths, parents):
@@ -323,6 +346,7 @@
     quarter = feature // TEAM
     heads = quarter // HD
     frames = enc_kv.shape[1]
+    pad = -(-(feature // HD) // 8) * 8
     bf, f32 = jnp.bfloat16, jnp.float32
     dma = pltpu.SemaphoreType.DMA
     hbm = pl.BlockSpec(memory_space=pl.ANY)
@@ -339,23 +363,19 @@
             pltpu.VMEM(cross_queries.shape, bf),
             pltpu.VMEM((frames, width), bf),
             pltpu.VMEM((n,) + parents.shape, jnp.int32),
-            pltpu.VMEM((rows, 1, feature), f32),
-            pltpu.VMEM((utts, 1, feature), f32),
-            pltpu.VMEM((utts, feature), f32),
+            pltpu.VMEM((rows, pad, HD), bf),
+            pltpu.VMEM((utts, pad, HD), bf),
+            pltpu.VMEM((utts * (feature // HD), HD), f32),
             pltpu.VMEM((heads, depth, TEAM, utts, HD), bf),
-            pltpu.VMEM((heads, depth, TEAM, utts, HD), bf),
-            pltpu.VMEM((heads, TEAM, utts, HD), bf),
-            pltpu.VMEM((TEAM, heads, utts, HD), bf),
-            pltpu.VMEM((n, utts, HD), bf),
+            pltpu.VMEM((heads, n, utts, HD), bf),
             pltpu.VMEM((n, 1, HD), f32),
             pltpu.VMEM((n, 1, HD), f32),
             pltpu.SMEM(lengths.shape, jnp.int32),
-            dma((7,)), dma((2 * heads,)), dma((n - 1,)), dma((n,)),
+            dma((7,)), dma((2 * heads,)), dma((TEAM - 1 + TEAM * (depth - 1),)), dma((n,)),
             dma((TEAM - 1 + TEAM * (depth - 1),)), dma((n,)),
             dma((2 * heads, TEAM - 1)), dma((2 * heads, TEAM)),
-            dma((n - 1,)), dma((n,)),
-            dma((heads, depth - 1)), dma((heads, depth)), dma((n - 1,)), dma((n,)),
-            dma((heads, TEAM - 1)), dma((TEAM, heads)), dma((n - 1,)), dma((n,)),
+            dma((n - 1,)), dma((n,)), dma((n - 1,)), dma((n,)),
+            dma((heads, n - 1)), dma((heads, n)), pltpu.SemaphoreType.REGULAR,
         ],
         compiler_params=pltpu.CompilerParams(
             collective_id=0, has_side_effects=True, vmem_limit_bytes=64 * 2**20 - 144 * 1024

time: 27 us -> 25.4 us (0.941)
  Pallas kernels: 25.6 us -> 24 us
    pallas_call x1, Pallas kernels: 25.6 us -> 24 us  [fast_body(): pl.pallas_call(functools.partial(fast_kernel, n), out_shape=pltpu.VMEM((u...]
where the time goes in v3:
time: 25.4 us; the launch traced here: 25.2 us
  Pallas kernels  24 us (94%)
  between operations  0.66 us (3%)
  local copies, waits for them, and re-layouts  0.62 us (2%)
    pallas_call x1, Pallas kernels, fast_body(): pl.pallas_call(functools.partial(fast_kernel, n), out_shape=pltpu.VMEM((u...  24 us
    unnamed x1, local copies, waits for them, and re-layouts  0.62 us

profile of v3, /device:TPU:0, one launch (start us, length us, event | category | flops | bytes accessed | tf_op | source)
XLA Modules:
  0.0 25.2 jit_solution(15886310202037387607)
XLA Ops:
  0.7 24.0 %shard_map.64 = bf16[16,1536]{1,0:T(8,128)(2,1)S(1)} custom-call(bf16[128,3072]{1,0:T(8,128)(2,1)} %bitcast.1, bf16[16,4608]{1,0:T(8,128)(2,1)} %new_ref.1, bf16[16,1536]{1,0:T(8,128)(2,1)} %cq_ref.1, bf16[1,256,3072]{2,1,0:T(8,128)(2,1)} %enc_ref.1, s32[1]{0:T(128)S(6)} %copy.9.len_ref, s32[1,16]{1,0:T(1,128)} %par_ref.1), custom_call_target="tpu_custom_call" | custom-call | tf_op jit(solution)/shard_map/pallas_call | solution.py:353
  24.6 0.6 %copy.8 = bf16[16,1536]{1,0:T(8,128)(2,1)} copy(bf16[16,1536]{1,0:T(8,128)(2,1)S(1)} %shard_map.64) | data formatting | bytes 98304

commit v4 on v3

--- a/solution.py
+++ b/solution.py
@@ -23,7 +23,7 @@
     out_ref,
     qbuf, kbuf, vbuf, newbuf, cqbuf, encbuf, ptab, xsend, xrecv, cross_ctx,
     ctx, gbuf, sstat, gstat, len_smem,
-    local_sem, own_sem, p_send, p_recv, q_send, q_recv, c_send, c_recv,
+    local_sem, own_sem, p_send, p_recv, pz_recv, q_send, q_recv, qz_recv, c_send, c_recv,
     x_send, x_recv, s_send, s_recv, g_send, g_recv, ready,
 ):
     feature = cq_ref.shape[1]
@@ -41,6 +41,9 @@
     z = me // TEAM
     r = me % TEAM
     others = [k + (k + depth - z) // depth for k in range(depth - 1)]
+    upper = 2 * z // depth
+    downward = [depth - 2 - k + (2 * depth - 2 - k - z) // depth for k in range(depth - 1)]
+    far_first = [upper * a + (1 - upper) * b for a, b in zip(others, downward)]
 
     def remote(src, dst, ssem, rsem, dev):
         return pltpu.make_async_remote_copy(
@@ -151,38 +154,7 @@
     live = lax.broadcasted_iota(jnp.int32, (rows, frames), 1) < len_smem[0]
     count_h = feature // HD
 
-    def pass_on(i):
-        src = z * TEAM + order[i]
-        piece = qbuf.at[src]
-        remote(piece, piece, q_send.at[0], q_recv.at[src], src).wait_recv()
-        remote(par_ref, ptab.at[src], p_send.at[0], p_recv.at[src], src).wait_recv()
-        for k, zz in enumerate(others):
-            spot = TEAM - 1 + (depth - 1) * (i + 1) + k
-            send(remote(piece, piece, q_send.at[spot], q_recv.at[src], zz * TEAM + r))
-            send(remote(ptab.at[src], ptab.at[src], p_send.at[spot], p_recv.at[src], zz * TEAM + r))
-
-    for h in range(count_h // 4):
-        cross(h, live)
-
-    @pl.when(core == 1)
-    def _():
-        pl.semaphore_wait(barrier, n - TEAM)
-        tell(ready, z * TEAM + partner)
-
-    @pl.when(core == 0)
-    def _():
-        pl.semaphore_wait(ready, 1)
-
-    for k, zz in enumerate(others):
-        send(remote(new_ref.at[:, cols(r * quarter, quarter)], qbuf.at[me],
-                    q_send.at[TEAM - 1 + k], q_recv.at[me], zz * TEAM + r))
-        send(remote(par_ref, ptab.at[me], p_send.at[TEAM - 1 + k], p_recv.at[me], zz * TEAM + r))
-    pass_on(TEAM - 2)
-    for h in range(count_h // 4, count_h // 2):
-        cross(h, live)
-    for i in far:
-        pass_on(i)
-    for h in range(count_h // 2, count_h):
+    for h in range(count_h):
         cross(h, live)
     pad = xsend.shape[1]
     to_row = lax.broadcasted_iota(jnp.int32, (rows * pad, rows * count_h), 0)
@@ -191,6 +163,31 @@
     turned = jnp.dot(turn.astype(jnp.bfloat16), jnp.concatenate(crossed, axis=0),
                      preferred_element_type=jnp.float32)
     xsend[...] = turned.astype(jnp.bfloat16).reshape(xsend.shape)
+    get_q.wait()
+    get_par.wait()
+    for rr in order:
+        src = z * TEAM + rr
+        remote(qbuf.at[src], qbuf.at[src], q_send.at[0], q_recv.at[src], src).wait_recv()
+        remote(par_ref, ptab.at[src], p_send.at[0], p_recv.at[src], src).wait_recv()
+
+    @pl.when(core == 1)
+    def _():
+        pl.semaphore_wait(barrier, n - TEAM)
+        tell(ready, z * TEAM + partner)
+
+    @pl.when(core == 0)
+    def _():
+        pl.semaphore_wait(ready, 1)
+
+    def shared(zz, to):
+        block = pl.ds(zz * TEAM, TEAM)
+        dev = to * TEAM + r
+        return [remote(ptab.at[block], ptab.at[block], p_send.at[TEAM - 1 + to], pz_recv.at[zz], dev),
+                remote(qbuf.at[block], qbuf.at[block], q_send.at[TEAM - 1 + to], qz_recv.at[zz], dev)]
+
+    for zz in far_first:
+        for cp in shared(z, zz):
+            send(cp)
     own_x = pltpu.make_async_copy(xsend.at[me], xrecv.at[me], local_sem.at[6])
     own_x.start()
 
@@ -198,17 +195,13 @@
         for k, dev in enumerate(devs):
             send(remote(xsend.at[dev], xrecv.at[me], x_send.at[at + k], x_recv.at[me], dev))
 
-    side = r // 2 * 2
-    near_x = [zz * TEAM + side + c for zz in others for c in range(2)] + [z * TEAM + partner]
-    far_x = [zz * TEAM + TEAM - 2 - side + c for zz in (*others, z) for c in range(2)]
-    send_x(near_x, 0)
-    send_x(far_x, len(near_x))
-
-    get_par.wait()
+    near = [(zz, rr) for zz in others for rr in (r, partner)] + [(z, partner)]
+    across = [(zz, rr) for zz in range(depth) for rr in order[:2]]
+    send_x([zz * TEAM + rr for zz, rr in near], 0)
+    send_x([zz * TEAM + rr for zz, rr in across[:2]], len(near))
+
     for zz in others:
-        for t in range(TEAM):
-            src = zz * TEAM + t
-            remote(par_ref, ptab.at[src], p_send.at[0], p_recv.at[src], src).wait_recv()
+        shared(zz, zz)[0].wait_recv()
     table = jnp.concatenate([ptab[u] for u in range(utts)], axis=0)
     beam_lane = lax.broadcasted_iota(jnp.int32, table.shape, 1)
     slot = jnp.concatenate(
@@ -227,12 +220,8 @@
         k = newbuf[:, feature + h * HD : feature + (h + 1) * HD].astype(jnp.float32)
         own.append(jnp.sum(q * k, axis=1, keepdims=True) * scale)
 
-    get_q.wait()
     for zz in others:
-        for t in range(TEAM):
-            src = zz * TEAM + t
-            piece = qbuf.at[src]
-            remote(piece, piece, q_send.at[0], q_recv.at[src], src).wait_recv()
+        shared(zz, zz)[1].wait_recv()
 
     def arrive(h, i):
         get_own[h][i].wait()
@@ -241,8 +230,7 @@
             remote(buf.at[h, rr], buf.at[h, rr], c_send.at[2 * h + i, 0], c_recv.at[2 * h + i, rr],
                    z * TEAM + rr).wait_recv()
 
-    team = [(zz, rr) for zz in others for rr in (r, partner, order[0], order[1])]
-    team += [(z, rr) for rr in order]
+    team = across[:2] + near + across[2:]
     stats = jnp.zeros((count, HD), jnp.float32)
     weight = []
 
@@ -262,26 +250,50 @@
             [jnp.where(slot == t, e, 0.0).astype(jnp.bfloat16) for t in range(TEAM)], axis=1))
         return jnp.where(spot == h * utts, jnp.where(here, m + jnp.log(total), 0.0), stats)
 
-    def give_back(h):
-        arrive(h, 1)
-        o = jnp.dot(weight[h], vbuf[h].reshape(TEAM * old, HD), preferred_element_type=jnp.float32)
-        ctx[h] = o.astype(jnp.bfloat16).reshape(depth, TEAM, utts, HD)
-        for k, (zz, rr) in enumerate(team):
+    def values(h, first, size):
+        o = jnp.dot(weight[h][first * span : (first + size) * span], vbuf[h].reshape(TEAM * old, HD),
+                    preferred_element_type=jnp.float32)
+        ctx[h, first : first + size] = o.astype(jnp.bfloat16).reshape(size, TEAM, utts, HD)
+
+    def give_back(h, picks):
+        for k in picks:
+            zz, rr = team[k]
             send(remote(ctx.at[h, zz, rr], gbuf.at[h, me], g_send.at[h, k], g_recv.at[h, me],
                         zz * TEAM + rr))
-        gbuf[h, pl.ds(me, 1)] = ctx[h, pl.ds(z, 1), pl.ds(r, 1)].reshape(1, utts, HD)
-
+
+    span = TEAM * utts
+    now = range(2 + len(near))
+    later = range(2 + len(near), n - 1)
+    held = []
     stats = score(0)
-    give_back(0)
     for h in range(1, heads):
+        if h == 1:
+            arrive(0, 1)
+            values(0, 0, depth)
+            give_back(0, now)
+            give_back(0, later) if False else held.append(0)
         stats = score(h)
     for g in range(n):
         sstat[g] = jnp.sum(stats[g * utts : (g + 1) * utts], axis=0, keepdims=True)
     for k, (zz, rr) in enumerate(team):
         send(remote(sstat.at[zz * TEAM + rr], gstat.at[me], s_send.at[k], s_recv.at[me], zz * TEAM + rr))
-    for h in range(1, heads):
-        give_back(h)
-
+    for h in range(1, last):
+        arrive(h, 1)
+        values(h, 0, depth)
+        give_back(h, now)
+        give_back(h, later) if False else held.append(h)
+    mark = len(sends)
+    arrive(last, 1)
+    values(last, 0, 1)
+    give_back(last, range(2))
+    values(last, 1, depth - 1)
+    give_back(last, range(2, n - 1)[: len(now) - 2])
+    for h in held:
+        give_back(h, later)
+    give_back(last, later)
+    send_x([zz * TEAM + rr for zz, rr in across[2:]], len(near) + 2)
+    for h in range(heads):
+        gbuf[h, pl.ds(me, 1)] = ctx[h, pl.ds(z, 1), pl.ds(r, 1)].reshape(1, utts, HD)
     gstat[pl.ds(me, 1)] = sstat[pl.ds(me, 1)]
 
     own_x.wait()
@@ -327,6 +339,8 @@
             self_ctx.astype(jnp.bfloat16).astype(jnp.float32) + cross_ctx[h * utts : (h + 1) * utts]
         ).astype(jnp.bfloat16)
 
+    for cp in sends[:mark]:
+        cp.wait_send()
     for hl in range(heads):
         for k in range(1, n):
             src = lax.rem(me + n - k, n)
@@ -334,7 +348,7 @@
         for t in range(TEAM):
             write(t, hl)
 
-    for cp in sends:
+    for cp in sends[mark:]:
         cp.wait_send()
 
 
@@ -371,8 +385,8 @@
             pltpu.VMEM((n, 1, HD), f32),
             pltpu.VMEM((n, 1, HD), f32),
             pltpu.SMEM(lengths.shape, jnp.int32),
-            dma((7,)), dma((2 * heads,)), dma((TEAM - 1 + TEAM * (depth - 1),)), dma((n,)),
-            dma((TEAM - 1 + TEAM * (depth - 1),)), dma((n,)),
+            dma((7,)), dma((2 * heads,)), dma((TEAM - 1 + depth,)), dma((n,)), dma((depth,)),
+            dma((TEAM - 1 + depth,)), dma((n,)), dma((depth,)),
             dma((2 * heads, TEAM - 1)), dma((2 * heads, TEAM)),
             dma((n - 1,)), dma((n,)), dma((n - 1,)), dma((n,)),
             dma((heads, n - 1)), dma((heads, n)), pltpu.SemaphoreType.REGULAR,

time: 25.4 us -> 24.2 us (0.953)
  Pallas kernels: 24 us -> 22.7 us
    pallas_call x1, Pallas kernels: 24 us -> 22.7 us  [fast_body(): pl.pallas_call(functools.partial(fast_kernel, n), out_shape=pltpu.VMEM((u...]
where the time goes in v4:
time: 24.2 us; the launch traced here: 24 us
  Pallas kernels  22.7 us (94%)
  between operations  0.66 us (3%)
  local copies, waits for them, and re-layouts  0.62 us (3%)
    pallas_call x1, Pallas kernels, fast_body(): pl.pallas_call(functools.partial(fast_kernel, n), out_shape=pltpu.VMEM((u...  22.7 us
    unnamed x1, local copies, waits for them, and re-layouts  0.62 us

profile of v4, /device:TPU:0, one launch (start us, length us, event | category | flops | bytes accessed | tf_op | source)
XLA Modules:
  0.0 24.0 jit_solution(2733155878657688538)
XLA Ops:
  0.7 22.7 %shard_map.64 = bf16[16,1536]{1,0:T(8,128)(2,1)S(1)} custom-call(bf16[128,3072]{1,0:T(8,128)(2,1)} %bitcast.1, bf16[16,4608]{1,0:T(8,128)(2,1)} %new_ref.1, bf16[16,1536]{1,0:T(8,128)(2,1)} %cq_ref.1, bf16[1,256,3072]{2,1,0:T(8,128)(2,1)} %enc_ref.1, s32[1]{0:T(128)S(6)} %copy.9.len_ref, s32[1,16]{1,0:T(1,128)} %par_ref.1), custom_call_target="tpu_custom_call" | custom-call | tf_op jit(solution)/shard_map/pallas_call | solution.py:367
  23.4 0.6 %copy.8 = bf16[16,1536]{1,0:T(8,128)(2,1)} copy(bf16[16,1536]{1,0:T(8,128)(2,1)S(1)} %shard_map.64) | data formatting | bytes 98304

commit v5 on v4

--- a/solution.py
+++ b/solution.py
@@ -23,8 +23,7 @@
     out_ref,
     qbuf, kbuf, vbuf, newbuf, cqbuf, encbuf, ptab, xsend, xrecv, cross_ctx,
     ctx, gbuf, sstat, gstat, len_smem,
-    local_sem, own_sem, p_send, p_recv, pz_recv, q_send, q_recv, qz_recv, c_send, c_recv,
-    x_send, x_recv, s_send, s_recv, g_send, g_recv, ready,
+    local_sem, own_sem, sent, got, c_recv, g_recv, ready,
 ):
     feature = cq_ref.shape[1]
     quarter = feature // TEAM
@@ -80,16 +79,11 @@
     get_q = pltpu.make_async_copy(new_ref.at[:, cols(r * quarter, quarter)], qbuf.at[me], local_sem.at[5])
     for cp in (get_len, get_cq, get_enc, get_q, get_par, get_new):
         cp.start()
-    get_own = []
     for h in range(heads):
-        pair = []
         for i, buf in enumerate((kbuf, vbuf)):
-            cp = pltpu.make_async_copy(
+            pltpu.make_async_copy(
                 cache_ref.at[:, cols(i * feature + r * quarter + h * HD, HD)], buf.at[h, r],
-                own_sem.at[2 * h + i])
-            cp.start()
-            pair.append(cp)
-        get_own.append(pair)
+                own_sem.at[i]).start()
 
     frames = encbuf.shape[0]
     ones_f = jnp.ones((frames, HD), jnp.bfloat16)
@@ -114,27 +108,29 @@
     def _():
         pl.semaphore_wait(ready, 1)
 
-    sends = []
-
-    def send(cp):
-        cp.start()
-        sends.append(cp)
-        return cp
+    def send(src, dst, ssem, rsem, dev):
+        remote(src, dst, sent.at[ssem], rsem, dev).start()
+
+    def receive(ref, rsem):
+        remote(ref, ref, sent.at[0], rsem, z * TEAM + partner).wait_recv()
+
+    def drain(ref, ssem):
+        remote(ref, ref, sent.at[ssem], got.at[0], z * TEAM + partner).wait_send()
 
     far = tuple(range(TEAM - 2))
     def ask(i):
-        send(remote(new_ref.at[:, cols(order[i] * quarter, quarter)], qbuf.at[me],
-                    q_send.at[i], q_recv.at[me], z * TEAM + order[i]))
-        send(remote(par_ref, ptab.at[me], p_send.at[i], p_recv.at[me], z * TEAM + order[i]))
+        dev = z * TEAM + order[i]
+        send(new_ref.at[:, cols(order[i] * quarter, quarter)], qbuf.at[me], 0, got.at[0], dev)
+        send(par_ref, ptab.at[me], 1, got.at[1], dev)
 
     for i in range(TEAM - 1):
         ask(i)
 
     def give(h, i, js):
         buf = (kbuf, vbuf)[i]
-        return [send(remote(cache_ref.at[:, cols(i * feature + order[j] * quarter + h * HD, HD)],
-                            buf.at[h, r], c_send.at[2 * h + i, j], c_recv.at[2 * h + i, r],
-                            z * TEAM + order[j])) for j in js]
+        for j in js:
+            send(cache_ref.at[:, cols(i * feature + order[j] * quarter + h * HD, HD)], buf.at[h, r],
+                 2 + i, c_recv.at[2 * h + i], z * TEAM + order[j])
 
     last = heads - 1
     give(0, 0, far)
@@ -163,45 +159,39 @@
     turned = jnp.dot(turn.astype(jnp.bfloat16), jnp.concatenate(crossed, axis=0),
                      preferred_element_type=jnp.float32)
     xsend[...] = turned.astype(jnp.bfloat16).reshape(xsend.shape)
-    get_q.wait()
-    get_par.wait()
-    for rr in order:
-        src = z * TEAM + rr
-        remote(qbuf.at[src], qbuf.at[src], q_send.at[0], q_recv.at[src], src).wait_recv()
-        remote(par_ref, ptab.at[src], p_send.at[0], p_recv.at[src], src).wait_recv()
 
     @pl.when(core == 1)
     def _():
         pl.semaphore_wait(barrier, n - TEAM)
         tell(ready, z * TEAM + partner)
 
+    get_q.wait()
+    get_par.wait()
+    receive(qbuf.at[pl.ds(0, TEAM - 1)], got.at[0])
+    receive(ptab.at[pl.ds(0, TEAM - 1)], got.at[1])
+
     @pl.when(core == 0)
     def _():
         pl.semaphore_wait(ready, 1)
 
-    def shared(zz, to):
-        block = pl.ds(zz * TEAM, TEAM)
-        dev = to * TEAM + r
-        return [remote(ptab.at[block], ptab.at[block], p_send.at[TEAM - 1 + to], pz_recv.at[zz], dev),
-                remote(qbuf.at[block], qbuf.at[block], q_send.at[TEAM - 1 + to], qz_recv.at[zz], dev)]
-
+    block = pl.ds(z * TEAM, TEAM)
     for zz in far_first:
-        for cp in shared(z, zz):
-            send(cp)
+        send(ptab.at[block], ptab.at[block], 1, got.at[3], zz * TEAM + r)
+        send(qbuf.at[block], qbuf.at[block], 0, got.at[2], zz * TEAM + r)
     own_x = pltpu.make_async_copy(xsend.at[me], xrecv.at[me], local_sem.at[6])
     own_x.start()
 
-    def send_x(devs, at):
-        for k, dev in enumerate(devs):
-            send(remote(xsend.at[dev], xrecv.at[me], x_send.at[at + k], x_recv.at[me], dev))
+    def send_x(picks):
+        for zz, rr in picks:
+            dev = zz * TEAM + rr
+            send(xsend.at[dev], xrecv.at[me], 4, got.at[4], dev)
 
     near = [(zz, rr) for zz in others for rr in (r, partner)] + [(z, partner)]
     across = [(zz, rr) for zz in range(depth) for rr in order[:2]]
-    send_x([zz * TEAM + rr for zz, rr in near], 0)
-    send_x([zz * TEAM + rr for zz, rr in across[:2]], len(near))
-
-    for zz in others:
-        shared(zz, zz)[0].wait_recv()
+    send_x(near)
+    send_x(across[:2])
+
+    receive(ptab.at[pl.ds(0, n - TEAM)], got.at[3])
     table = jnp.concatenate([ptab[u] for u in range(utts)], axis=0)
     beam_lane = lax.broadcasted_iota(jnp.int32, table.shape, 1)
     slot = jnp.concatenate(
@@ -220,15 +210,14 @@
         k = newbuf[:, feature + h * HD : feature + (h + 1) * HD].astype(jnp.float32)
         own.append(jnp.sum(q * k, axis=1, keepdims=True) * scale)
 
-    for zz in others:
-        shared(zz, zz)[1].wait_recv()
+    receive(qbuf.at[pl.ds(0, n - TEAM)], got.at[2])
 
     def arrive(h, i):
-        get_own[h][i].wait()
         buf = (kbuf, vbuf)[i]
-        for rr in order:
-            remote(buf.at[h, rr], buf.at[h, rr], c_send.at[2 * h + i, 0], c_recv.at[2 * h + i, rr],
-                   z * TEAM + rr).wait_recv()
+        if h == 0:
+            mine = buf.at[:, pl.ds(r, 1)]
+            pltpu.make_async_copy(mine, mine, own_sem.at[i]).wait()
+        receive(buf.at[h, pl.ds(0, TEAM - 1)], c_recv.at[2 * h + i])
 
     team = across[:2] + near + across[2:]
     stats = jnp.zeros((count, HD), jnp.float32)
@@ -258,8 +247,7 @@
     def give_back(h, picks):
         for k in picks:
             zz, rr = team[k]
-            send(remote(ctx.at[h, zz, rr], gbuf.at[h, me], g_send.at[h, k], g_recv.at[h, me],
-                        zz * TEAM + rr))
+            send(ctx.at[h, zz, rr], gbuf.at[h, me], 5, g_recv.at[h], zz * TEAM + rr)
 
     span = TEAM * utts
     now = range(2 + len(near))
@@ -271,44 +259,39 @@
             arrive(0, 1)
             values(0, 0, depth)
             give_back(0, now)
-            give_back(0, later) if False else held.append(0)
+            held.append(0)
         stats = score(h)
     for g in range(n):
         sstat[g] = jnp.sum(stats[g * utts : (g + 1) * utts], axis=0, keepdims=True)
-    for k, (zz, rr) in enumerate(team):
-        send(remote(sstat.at[zz * TEAM + rr], gstat.at[me], s_send.at[k], s_recv.at[me], zz * TEAM + rr))
+    for zz, rr in team:
+        send(sstat.at[zz * TEAM + rr], gstat.at[me], 6, got.at[5], zz * TEAM + rr)
     for h in range(1, last):
         arrive(h, 1)
         values(h, 0, depth)
         give_back(h, now)
-        give_back(h, later) if False else held.append(h)
-    mark = len(sends)
+        held.append(h)
     arrive(last, 1)
     values(last, 0, 1)
     give_back(last, range(2))
     values(last, 1, depth - 1)
-    give_back(last, range(2, n - 1)[: len(now) - 2])
+    give_back(last, range(2, 2 + len(near)))
+    send_x(across[2:])
     for h in held:
         give_back(h, later)
     give_back(last, later)
-    send_x([zz * TEAM + rr for zz, rr in across[2:]], len(near) + 2)
     for h in range(heads):
         gbuf[h, pl.ds(me, 1)] = ctx[h, pl.ds(z, 1), pl.ds(r, 1)].reshape(1, utts, HD)
     gstat[pl.ds(me, 1)] = sstat[pl.ds(me, 1)]
 
     own_x.wait()
-    for k in range(1, n):
-        src = lax.rem(me + n - k, n)
-        remote(xsend.at[src], xrecv.at[src], x_send.at[0], x_recv.at[src], src).wait_recv()
+    receive(xrecv.at[pl.ds(0, n - 1)], got.at[4])
     to_row = lax.broadcasted_iota(jnp.int32, (utts * count_h, utts * pad), 0)
     from_row = lax.broadcasted_iota(jnp.int32, (utts * count_h, utts * pad), 1)
     turn = (to_row % utts == from_row // pad) & (to_row // utts == from_row % pad)
     cross_ctx[...] = jnp.dot(turn.astype(jnp.bfloat16), xrecv[...].reshape(utts * pad, HD),
                              preferred_element_type=jnp.float32)
 
-    for k in range(1, n):
-        src = lax.rem(me + n - k, n)
-        remote(gstat.at[src], gstat.at[src], s_send.at[0], s_recv.at[src], src).wait_recv()
+    receive(gstat.at[pl.ds(0, n - 1)], got.at[5])
     weights = []
     f_lane = lax.broadcasted_iota(jnp.int32, (utts, HD), 1)
     f_row = lax.broadcasted_iota(jnp.int32, (utts, HD), 0)
@@ -339,17 +322,19 @@
             self_ctx.astype(jnp.bfloat16).astype(jnp.float32) + cross_ctx[h * utts : (h + 1) * utts]
         ).astype(jnp.bfloat16)
 
-    for cp in sends[:mark]:
-        cp.wait_send()
+    most = pl.ds(0, n - 1)
     for hl in range(heads):
-        for k in range(1, n):
-            src = lax.rem(me + n - k, n)
-            remote(gbuf.at[hl, src], gbuf.at[hl, src], g_send.at[hl, 0], g_recv.at[hl, src], src).wait_recv()
+        if hl == last:
+            drain(qbuf.at[most], 0)
+            drain(ptab.at[most], 1)
+            drain(kbuf.at[:, pl.ds(0, TEAM - 1)], 2)
+            drain(vbuf.at[:, pl.ds(0, TEAM - 1)], 3)
+            drain(xrecv.at[most], 4)
+            drain(gbuf.at[:, most], 5)
+            drain(gstat.at[most], 6)
+        receive(gbuf.at[hl, most], g_recv.at[hl])
         for t in range(TEAM):
             write(t, hl)
-
-    for cp in sends[mark:]:
-        cp.wait_send()
 
 
 def fast_body(n, cache_kv, new_rows, cross_queries, enc_kv, lengths, parents):
@@ -385,11 +370,8 @@
             pltpu.VMEM((n, 1, HD), f32),
             pltpu.VMEM((n, 1, HD), f32),
             pltpu.SMEM(lengths.shape, jnp.int32),
-            dma((7,)), dma((2 * heads,)), dma((TEAM - 1 + depth,)), dma((n,)), dma((depth,)),
-            dma((TEAM - 1 + depth,)), dma((n,)), dma((depth,)),
-            dma((2 * heads, TEAM - 1)), dma((2 * heads, TEAM)),
-            dma((n - 1,)), dma((n,)), dma((n - 1,)), dma((n,)),
-            dma((heads, n - 1)), dma((heads, n)), pltpu.SemaphoreType.REGULAR,
+            dma((7,)), dma((2,)), dma((7,)), dma((6,)), dma((2 * heads,)), dma((heads,)),
+            pltpu.SemaphoreType.REGULAR,
         ],
         compiler_params=pltpu.CompilerParams(
             collective_id=0, has_side_effects=True, vmem_limit_bytes=64 * 2**20 - 144 * 1024

time: 24.2 us -> 22 us (0.909)
  Pallas kernels: 22.7 us -> 20.6 us
    pallas_call x1, Pallas kernels: 22.7 us -> 20.6 us  [fast_body(): pl.pallas_call(functools.partial(fast_kernel, n), out_shape=pltpu.VMEM((u...]
where the time goes in v5:
time: 22 us; the launch traced here: 21.8 us
  Pallas kernels  20.6 us (94%)
  between operations  0.66 us (3%)
  local copies, waits for them, and re-layouts  0.62 us (3%)
    pallas_call x1, Pallas kernels, fast_body(): pl.pallas_call(functools.partial(fast_kernel, n), out_shape=pltpu.VMEM((u...  20.6 us
    unnamed x1, local copies, waits for them, and re-layouts  0.62 us

profile of v5, /device:TPU:0, one launch (start us, length us, event | category | flops | bytes accessed | tf_op | source)
XLA Modules:
  0.0 21.8 jit_solution(2091569803608758124)
XLA Ops:
  0.7 20.6 %shard_map.64 = bf16[16,1536]{1,0:T(8,128)(2,1)S(1)} custom-call(bf16[128,3072]{1,0:T(8,128)(2,1)} %bitcast.1, bf16[16,4608]{1,0:T(8,128)(2,1)} %new_ref.1, bf16[16,1536]{1,0:T(8,128)(2,1)} %cq_ref.1, bf16[1,256,3072]{2,1,0:T(8,128)(2,1)} %enc_ref.1, s32[1]{0:T(128)S(6)} %copy.9.len_ref, s32[1,16]{1,0:T(1,128)} %par_ref.1), custom_call_target="tpu_custom_call" | custom-call | tf_op jit(solution)/shard_map/pallas_call | solution.py:352
  21.2 0.6 %copy.8 = bf16[16,1536]{1,0:T(8,128)(2,1)} copy(bf16[16,1536]{1,0:T(8,128)(2,1)S(1)} %shard_map.64) | data formatting | bytes 98304

commit v6 on v5

--- a/solution.py
+++ b/solution.py
@@ -64,6 +64,14 @@
     def _():
         tell(barrier, z * TEAM + partner)
 
+    @pl.when(upper == 1)
+    def _():
+        tell(barrier, z * TEAM + lax.rem(r - core + 1 + CORES, TEAM))
+
+    @pl.when(upper * (1 - core) == 1)
+    def _():
+        tell(barrier, z * TEAM + partner)
+
     for zz in others:
         for t in range(1, TEAM, CORES):
             tell(barrier, zz * TEAM + t)
@@ -102,11 +110,19 @@
     @pl.when(core == 0)
     def _():
         pl.semaphore_wait(barrier, TEAM - 1)
+
+        @pl.when(upper == 0)
+        def _():
+            tell(ready, z * TEAM + partner)
+
+    @pl.when(core * (1 - upper) == 1)
+    def _():
+        pl.semaphore_wait(ready, 1)
+
+    @pl.when(core * upper == 1)
+    def _():
+        pl.semaphore_wait(barrier, n - 1)
         tell(ready, z * TEAM + partner)
-
-    @pl.when(core == 1)
-    def _():
-        pl.semaphore_wait(ready, 1)
 
     def send(src, dst, ssem, rsem, dev):
         remote(src, dst, sent.at[ssem], rsem, dev).start()
@@ -160,7 +176,7 @@
                      preferred_element_type=jnp.float32)
     xsend[...] = turned.astype(jnp.bfloat16).reshape(xsend.shape)
 
-    @pl.when(core == 1)
+    @pl.when(core * (1 - upper) == 1)
     def _():
         pl.semaphore_wait(barrier, n - TEAM)
         tell(ready, z * TEAM + partner)

time: 22 us -> 21.9 us (level)
  no operation moved by 1% of the time
where the time goes in v6:
time: 21.9 us; the launch traced here: 21.7 us
  Pallas kernels  20.5 us (94%)
  between operations  0.66 us (3%)
  local copies, waits for them, and re-layouts  0.62 us (3%)
    pallas_call x1, Pallas kernels, fast_body(): pl.pallas_call(functools.partial(fast_kernel, n), out_shape=pltpu.VMEM((u...  20.5 us
    unnamed x1, local copies, waits for them, and re-layouts  0.62 us

profile of v6, /device:TPU:0, one launch (start us, length us, event | category | flops | bytes accessed | tf_op | source)
XLA Modules:
  0.0 21.7 jit_solution(15644302946831272469)
XLA Ops:
  0.7 20.5 %shard_map.64 = bf16[16,1536]{1,0:T(8,128)(2,1)S(1)} custom-call(bf16[128,3072]{1,0:T(8,128)(2,1)} %bitcast.1, bf16[16,4608]{1,0:T(8,128)(2,1)} %new_ref.1, bf16[16,1536]{1,0:T(8,128)(2,1)} %cq_ref.1, bf16[1,256,3072]{2,1,0:T(8,128)(2,1)} %enc_ref.1, s32[1]{0:T(128)S(6)} %copy.9.len_ref, s32[1,16]{1,0:T(1,128)} %par_ref.1), custom_call_target="tpu_custom_call" | custom-call | tf_op jit(solution)/shard_map/pallas_call | solution.py:368
  21.1 0.6 %copy.8 = bf16[16,1536]{1,0:T(8,128)(2,1)} copy(bf16[16,1536]{1,0:T(8,128)(2,1)S(1)} %shard_map.64) | data formatting | bytes 98304
